TPU v7x, 32 devices: a whole 2x2x4 slice. The times are simulated.
32 devices in a mesh: groups: 2 (over y), row: 8 (over z, x), col: 2 (over core).
Axes of the slice: x: 2, y: 2, z: 4, core: 2. Of those that a mesh axis runs over, the one named last changes fastest.
Arguments:
- wavenumber: float32 [2], P('groups'), parts along dimension 0, may hold values from 30 to 90
- tgt_geom: float32 [6, 4096], P(None, ('groups', 'row')), parts along dimension 1, may hold values from -2 to 8, as said below
- src_geom: float32 [4, 512], P(None, ('groups', 'row', 'col')), parts along dimension 1, may hold values from -2 to 8, as said below
- excite: bfloat16 [128, 512], P(None, ('groups', 'row', 'col')), parts along dimension 1, may hold values from -6 to 6
- tgt_nodes: float32 [3, 6144], P(None, ('groups', 'row')), parts along dimension 1, may hold values from -2 to 8, as said below
- src_nodes: float32 [3, 3072], P(None, ('groups', 'row')), parts along dimension 1, may hold values from -2 to 8, as said below
- tgt_weights: bfloat16 [2, 192, 4096], P(None, None, ('groups', 'row')), parts along dimension 2, may hold values from -0.109375 to 0.109375
- src_weights: bfloat16 [2, 192, 512], P(None, None, ('groups', 'row', 'col')), parts along dimension 2, may hold values from -1 to 1
- near_order: int32 [32, 9], P(('groups', 'row')), parts along dimension 0, may hold values from 0 to 3
Outputs:
- responses: float32 [4096, 128], P(('groups', 'row', 'col')), parts along dimension 0
There are 2 independent parts, one for each index of `groups`. A program takes and returns all parts, laid end to end along the dimension named above; each array names one. Nothing has to cross between parts.
Inputs may be any that keep to these rules, and one draw needn't show every extreme that they name: `tgt_geom`: rows 0 to 2 are points, rows 3 to 5 unit normals. `src_geom`: rows 0 to 2 are points, row 3 positive areas. `tgt_nodes`: Points. `src_nodes`: Points. `near_order`: 0 marks a pair that is not near.
All inputs are finite; a program needn't handle non-finite values.
Results may differ from a plain program's by a relative error of at most 0.0011.
Values may be sent and summed in bfloat16 or wider, within the bound.
A program may use at most 64 MiB of HBM per device.

v0:
```python
import functools
import math

import jax
import jax.numpy as jnp
import numpy as np
from jax import lax
from jax.experimental import pallas as pl
from jax.experimental.pallas import tpu as pltpu
from jax.sharding import PartitionSpec as P

ORDERS = 3
SOFT = 0.05
FOUR_PI = 4.0 * math.pi
LANES = 128
MESH = pl.DeviceIdType.MESH
TN = (((0,), (0,)), ((), ()))
NT = (((1,), (1,)), ((), ()))


def fitted(function, terms):
    nodes = (np.cos((np.arange(terms) + 0.5) * np.pi / terms) + 1.0) / 8.0
    matrix = np.vander(nodes, terms, increasing=True)
    return [float(c) for c in np.linalg.solve(matrix, function(np.sqrt(nodes)))]


COS = fitted(lambda u: np.cos(2.0 * np.pi * u), 7)
SIN = fitted(lambda u: np.sin(2.0 * np.pi * u) / u, 7)


def horner(coefficients, y):
    total = coefficients[-1]
    for c in coefficients[-2::-1]:
        total = total * y + c
    return total


def cos_sin(turns):
    u = turns - jnp.round(turns)
    y = u * u
    return horner(COS, y), u * horner(SIN, y)


def times_i(value):
    half = value.shape[1] // 2
    swapped = jnp.concatenate([value[:, half:], value[:, :half]], 1)
    lane = lax.broadcasted_iota(jnp.int32, value.shape, 1)
    return jnp.where(lane < half, -swapped, swapped)


def split_two(value):
    high = value.astype(jnp.bfloat16)
    return high, (value - high.astype(jnp.float32)).astype(jnp.bfloat16)


def columns_of(rows):
    few, lanes = rows.shape
    pad = jnp.zeros((8 - few, lanes), jnp.float32)
    return jnp.concatenate([rows, pad], 0).T


def kernel(
    wave_hbm,
    order_hbm,
    tgt_hbm,
    tnode_hbm,
    tweight_hbm,
    geom_hbm,
    excite_hbm,
    snode_hbm,
    sweight_hbm,
    out_ref,
    node_all,
    weight_all,
    geom_all,
    excite_all,
    green_high,
    green_low,
    wave_ref,
    order_ref,
    tgt_ref,
    tnode_ref,
    tweight_ref,
    node_own,
    local,
    node_send,
    weight_send,
    geom_send,
    excite_send,
    recv,
    weight_recv,
    weight_pair,
    weight_back,
    pair_send,
    pair_recv,
):
    n_row = lax.axis_size("row")
    row = lax.axis_index("row")
    col = lax.axis_index("col")
    other = 1 - col
    band = node_all.shape[0]
    reach = (band - 1) // 2
    qn = node_all.shape[2]
    qpad = pl.cdiv(qn, LANES) * LANES
    step_nodes = qn // ORDERS
    per = excite_hbm.shape[0]
    blk = out_ref.shape[0]

    barrier = pltpu.get_barrier_semaphore()

    @pl.loop(1, n_row)
    def _(d):
        pl.semaphore_signal(
            barrier, inc=1, device_id={"row": lax.rem(row + d, n_row)}, device_id_type=MESH
        )

    pl.semaphore_signal(barrier, inc=1, device_id={"col": other}, device_id_type=MESH)

    loads = [
        pltpu.make_async_copy(here, there, local.at[index])
        for index, (here, there) in enumerate(
            (
                (wave_hbm, wave_ref),
                (tnode_hbm, tnode_ref),
                (order_hbm, order_ref),
                (tgt_hbm, tgt_ref),
                (tweight_hbm, tweight_ref),
            )
        )
    ]
    own_nodes = pltpu.make_async_copy(snode_hbm, node_own, local.at[len(loads)])
    own_nodes.start()
    for load in loads:
        load.start()

    def fill(slot):
        pltpu.make_async_copy(snode_hbm, node_all.at[slot], recv.at[0]).start()
        pltpu.make_async_copy(sweight_hbm, weight_all.at[col, slot], weight_recv.at[slot]).start()

    @pl.loop(0, band)
    def _(slot):
        block = row + slot - reach
        missing = jnp.logical_or(block < 0, block >= n_row)

        @pl.when(jnp.logical_or(missing, slot == reach))
        def _():
            fill(slot)

    pltpu.make_async_copy(geom_hbm, geom_all.at[col, row], recv.at[2]).start()
    pltpu.make_async_copy(excite_hbm, excite_all.at[col, row], recv.at[3]).start()

    def near_copies(slot):
        to = {"row": row + reach - slot}
        nodes = pltpu.make_async_remote_copy(
            src_ref=snode_hbm,
            dst_ref=node_all.at[slot],
            send_sem=node_send.at[slot],
            recv_sem=recv.at[0],
            device_id=to,
            device_id_type=MESH,
        )
        weights = pltpu.make_async_remote_copy(
            src_ref=sweight_hbm,
            dst_ref=weight_all.at[col, slot],
            send_sem=weight_send.at[slot],
            recv_sem=weight_recv.at[slot],
            device_id=to,
            device_id_type=MESH,
        )
        return nodes, weights

    def far_copies(d):
        to = {"row": lax.rem(row + d, n_row)}
        geoms = pltpu.make_async_remote_copy(
            src_ref=geom_hbm,
            dst_ref=geom_all.at[col, row],
            send_sem=geom_send.at[d],
            recv_sem=recv.at[2],
            device_id=to,
            device_id_type=MESH,
        )
        excites = pltpu.make_async_remote_copy(
            src_ref=excite_hbm,
            dst_ref=excite_all.at[col, row],
            send_sem=excite_send.at[d],
            recv_sem=recv.at[3],
            device_id=to,
            device_id_type=MESH,
        )
        return geoms, excites

    def for_near(act):
        @pl.loop(0, band)
        def _(slot):
            goal = row + reach - slot
            inside = jnp.logical_and(goal >= 0, goal < n_row)

            @pl.when(jnp.logical_and(inside, slot != reach))
            def _():
                act(slot)

    def weight_to_pair(slot, half):
        return pltpu.make_async_remote_copy(
            src_ref=weight_all.at[half, slot],
            dst_ref=weight_all.at[half, slot],
            send_sem=weight_pair.at[slot],
            recv_sem=weight_back.at[slot],
            device_id={"col": other},
            device_id_type=MESH,
        )

    def to_pair(index, buffer):
        return pltpu.make_async_remote_copy(
            src_ref=buffer.at[col],
            dst_ref=buffer.at[col],
            send_sem=pair_send.at[index],
            recv_sem=pair_recv.at[index],
            device_id={"col": other},
            device_id_type=MESH,
        )

    def from_pair(index, buffer):
        return pltpu.make_async_remote_copy(
            src_ref=buffer.at[other],
            dst_ref=buffer.at[other],
            send_sem=pair_send.at[index],
            recv_sem=pair_recv.at[index],
            device_id={"col": other},
            device_id_type=MESH,
        )

    for load in loads[:3]:
        load.wait()
    wave = wave_ref[0]
    per_turn = wave * (0.5 / math.pi)

    tnodes = tnode_ref[...]
    tnodes = jnp.where(col == 0, tnodes[:, :qn], tnodes[:, qn:])
    if qpad > qn:
        tnodes = jnp.concatenate([tnodes, jnp.zeros((3, qpad - qn), jnp.float32)], 1)
    tcols = columns_of(tnodes)[:qn]
    t_x, t_y, t_z = (jnp.broadcast_to(tcols[:, i : i + 1], (qn, LANES)) for i in range(3))

    point = lax.broadcasted_iota(jnp.int32, (qn, LANES), 0)

    def order_of(slot):
        block = row + slot - reach
        valid = jnp.logical_and(block >= 0, block < n_row)
        return jnp.where(valid, order_ref[col, slot] * step_nodes, 0)

    def green_of(slot, snodes):
        live = point < order_of(slot)
        if qpad > qn:
            snodes = jnp.concatenate([snodes, jnp.zeros((3, qpad - qn), jnp.float32)], 1)
        for part in range(qpad // LANES):
            here = slice(part * LANES, (part + 1) * LANES)
            d_x = t_x - snodes[0:1, here]
            d_y = t_y - snodes[1:2, here]
            d_z = t_z - snodes[2:3, here]
            squared = d_x * d_x + d_y * d_y + d_z * d_z + SOFT * SOFT
            inverse = lax.rsqrt(squared)
            cosine, sine = cos_sin(per_turn * (squared * inverse))
            inverse = jnp.where(live, inverse, 0.0)
            for index, value in enumerate((inverse * cosine, inverse * sine)):
                high, low = split_two(value)
                at = pl.multiple_of((2 * slot + index) * qpad + part * LANES, LANES)
                green_high[:, pl.ds(at, LANES)] = high
                green_low[:, pl.ds(at, LANES)] = low

    own_nodes.wait()
    green_of(reach, node_own[...])

    pl.semaphore_wait(barrier, n_row)

    for_near(lambda slot: near_copies(slot)[0].start())

    @pl.loop(1, n_row)
    def _(d):
        far_copies(d)[0].start()

    for_near(lambda slot: near_copies(slot)[1].start())

    @pl.loop(1, n_row)
    def _(d):
        far_copies(d)[1].start()

    pltpu.make_async_copy(node_all, node_all, recv.at[0]).wait()

    def green_some(begin, end):
        @pl.loop(begin, end)
        def _(slot):
            block = row + slot - reach
            needed = jnp.logical_and(block >= 0, block < n_row)

            @pl.when(jnp.logical_and(needed, slot != reach))
            def _():
                green_of(slot, node_all[slot])

            @pl.when(jnp.logical_not(needed))
            def _():
                at = pl.ds(pl.multiple_of(2 * slot * qpad, LANES), 2 * qpad)
                green_high[:, at] = jnp.zeros((qn, 2 * qpad), jnp.bfloat16)
                green_low[:, at] = jnp.zeros((qn, 2 * qpad), jnp.bfloat16)

    green_some(0, (band - 2))
    pltpu.make_async_copy(geom_all.at[col], geom_all.at[col], recv.at[2]).wait()
    to_pair(0, geom_all).start()

    @pl.loop(0, band)
    def _(slot):
        pltpu.make_async_copy(
            weight_all.at[col, slot], weight_all.at[col, slot], weight_recv.at[slot]
        ).wait()
        weight_to_pair(slot, col).start()

    pltpu.make_async_copy(excite_all.at[col], excite_all.at[col], recv.at[3]).wait()
    to_pair(1, excite_all).start()
    green_some((band - 2), band)
    from_pair(0, geom_all).wait_recv()

    loads[3].wait()
    begin = pl.multiple_of(col * blk, blk)
    gcols = columns_of(tgt_ref[:, pl.ds(begin, blk)])
    p_x, p_y, p_z, n_x, n_y, n_z = (gcols[:, i : i + 1] for i in range(6))
    pieces = LANES // per
    chunks = n_row // pieces

    def impedance(half, chunk):
        places = jnp.concatenate([geom_all[half, chunk * pieces + i] for i in range(pieces)], 1)
        d_x = p_x - places[0:1]
        d_y = p_y - places[1:2]
        d_z = p_z - places[2:3]
        squared = d_x * d_x + d_y * d_y + d_z * d_z + SOFT * SOFT
        inverse = lax.rsqrt(squared)
        radius = squared * inverse
        along = (n_x * d_x + n_y * d_y + n_z * d_z) * inverse
        scale = places[3:4] * (inverse * (1.0 / FOUR_PI))
        cosine, sine = cos_sin(per_turn * radius)
        green_re = scale * cosine
        green_im = scale * sine
        factor_re = 1.0 - along
        factor_im = -along / (wave * radius)
        kern_re = green_re * factor_re - green_im * factor_im
        kern_im = green_re * factor_im + green_im * factor_re
        return jnp.concatenate(
            [kern_re.astype(jnp.bfloat16), kern_im.astype(jnp.bfloat16)], 1
        )

    def both(rows):
        turned = times_i(rows.astype(jnp.float32)).astype(jnp.bfloat16)
        return jnp.concatenate([rows, turned], 0)

    from_pair(1, excite_all).wait_recv()

    def far_step(index, total):
        half, chunk = index // chunks, lax.rem(index, chunks)
        rows = excite_all[half, pl.ds(chunk * pieces, pieces)].reshape(LANES, blk)
        return total + jnp.dot(
            impedance(half, chunk), both(rows), preferred_element_type=jnp.float32
        )

    far = lax.fori_loop(0, 2 * chunks, far_step, jnp.zeros(out_ref.shape, jnp.float32))

    width = out_ref.shape[1]

    lane = lax.broadcasted_iota(jnp.int32, (2 * per, qpad), 1)
    applied, sources = [], []
    for slot in range(band):
        weight_to_pair(slot, other).wait_recv()
        live = lane < order_of(slot)
        basis = []
        for part in range(2):
            value = jnp.concatenate([weight_all[half, slot, part] for half in range(2)], 0)
            if qpad > qn:
                value = jnp.concatenate(
                    [value, jnp.zeros((2 * per, qpad - qn), jnp.bfloat16)], 1
                )
            basis.append(jnp.where(live, value.astype(jnp.float32), 0.0))
        stacked = jnp.concatenate(
            [
                jnp.concatenate([basis[0], -basis[1]], 1),
                jnp.concatenate([basis[1], basis[0]], 1),
            ],
            0,
        ).astype(jnp.bfloat16)
        here = slice(2 * slot * qpad, 2 * (slot + 1) * qpad)
        applied.append(
            lax.dot_general(green_high[:, here], stacked, NT, preferred_element_type=jnp.float32)
            + lax.dot_general(green_low[:, here], stacked, NT, preferred_element_type=jnp.float32)
        )
        source = jnp.clip(row + slot - reach, 0, n_row - 1)
        sources.append(both(jnp.concatenate([excite_all[half, source] for half in range(2)], 0)))
    high, low = split_two(jnp.concatenate(applied, 1))
    sources = jnp.concatenate(sources, 0)
    inner = jnp.dot(high, sources, preferred_element_type=jnp.float32) + jnp.dot(
        low, sources, preferred_element_type=jnp.float32
    )
    inner = inner * (1.0 / FOUR_PI)
    loads[4].wait()
    tests = jnp.concatenate(
        [tweight_ref[0, :, pl.ds(begin, blk)], tweight_ref[1, :, pl.ds(begin, blk)]], 0
    )
    high, low = split_two(jnp.concatenate([inner, times_i(inner)], 0))
    product = lax.dot_general(
        tests, jnp.concatenate([high, low], 1), TN, preferred_element_type=jnp.float32
    )
    out_ref[...] = far + (product[:, :width] + product[:, width:])

    for_near(lambda slot: [copy.wait_send() for copy in near_copies(slot)])

    @pl.loop(1, n_row)
    def _(d):
        for copy in far_copies(d):
            copy.wait_send()

    @pl.loop(0, band)
    def _(slot):
        weight_to_pair(slot, col).wait_send()

    for index, buffer in enumerate((geom_all, excite_all)):
        to_pair(index, buffer).wait_send()


def on_device(
    wavenumber,
    tgt_geom,
    src_geom,
    excite,
    tgt_nodes,
    src_nodes,
    tgt_weights,
    src_weights,
    near_order,
):
    n_row = lax.axis_size("row")
    band = near_order.shape[1]
    blk = tgt_geom.shape[1] // lax.axis_size("col")
    qn = src_nodes.shape[1]
    qpad = -(-qn // LANES) * LANES
    excite_rows = excite.T
    weight_rows = src_weights.transpose(0, 2, 1)
    vmem = pl.BlockSpec(memory_space=pltpu.VMEM)
    hbm = pl.BlockSpec(memory_space=pl.ANY)
    dma = pltpu.SemaphoreType.DMA
    return pl.pallas_call(
        kernel,
        out_shape=jax.ShapeDtypeStruct((blk, excite.shape[0]), jnp.float32),
        in_specs=[hbm] * 9,
        out_specs=vmem,
        scratch_shapes=[
            pltpu.VMEM((band,) + src_nodes.shape, jnp.float32),
            pltpu.VMEM((2, band) + weight_rows.shape, jnp.bfloat16),
            pltpu.VMEM((2, n_row) + src_geom.shape, jnp.float32),
            pltpu.VMEM((2, n_row) + excite_rows.shape, jnp.bfloat16),
            pltpu.VMEM((qn, band * 2 * qpad), jnp.bfloat16),
            pltpu.VMEM((qn, band * 2 * qpad), jnp.bfloat16),
            pltpu.SMEM(wavenumber.shape, jnp.float32),
            pltpu.SMEM(near_order.shape, jnp.int32),
            pltpu.VMEM(tgt_geom.shape, jnp.float32),
            pltpu.VMEM(tgt_nodes.shape, jnp.float32),
            pltpu.VMEM(tgt_weights.shape, jnp.bfloat16),
            pltpu.VMEM(src_nodes.shape, jnp.float32),
            dma((6,)),
            dma((band,)),
            dma((band,)),
            dma((n_row,)),
            dma((n_row,)),
            dma((4,)),
            dma((band,)),
            dma((band,)),
            dma((band,)),
            dma((2,)),
            dma((2,)),
        ],
        compiler_params=pltpu.CompilerParams(collective_id=0, has_side_effects=True),
        name="slab",
    )(
        wavenumber,
        near_order,
        tgt_geom,
        tgt_nodes,
        tgt_weights,
        src_geom,
        excite_rows,
        src_nodes,
        weight_rows,
    )


def solution(mesh):
    return jax.shard_map(
        on_device,
        mesh=mesh,
        in_specs=(
            P("groups"),
            P(None, ("groups", "row")),
            P(None, ("groups", "row", "col")),
            P(None, ("groups", "row", "col")),
            P(None, ("groups", "row")),
            P(None, ("groups", "row")),
            P(None, None, ("groups", "row")),
            P(None, None, ("groups", "row", "col")),
            P(("groups", "row"), None),
        ),
        out_specs=P(("groups", "row", "col"), None),
        check_vma=False,
    )
```

profile of v0, /device:TPU:0, one launch (start us, length us, event | category | flops | bytes accessed | tf_op | source)
XLA Modules:
  0.0 19.8 jit_solution(326420298280583003)
XLA Ops:
  0.7 17.6 %slab.1 = f32[128,128]{1,0:T(8,128)} custom-call(f32[1]{0:T(128)S(6)} %copy.11.wave_hbm, s32[2,9]{1,0:T(2,128)} %order_hbm.1, f32[6,256]{1,0:T(8,128)} %tgt_hbm.1, f32[3,384]{1,0:T(4,128)} %tnode_hbm.1, bf16[2,192,256]{2,1,0:T(8,128)(2,1)} %tweight_hbm.1, f32[4,16]{1,0:T(4,128)} %geom_hbm.1, bf16[16,128]{1,0:T(8,128)(2,1)} %bitcast.3, f32[3,192]{1,0:T(4,128)} %snode_hbm.1, ...), custom_call_target="tpu_custom_call" | custom-call | tf_op jit(solution)/shard_map/slab/pallas_call | solution.py:445
  18.3 1.5 %copy.12 = f32[128,128]{1,0:T(8,128)} copy(f32[128,128]{1,0:T(8,128)} %slab.1) | data formatting | bytes 131072
where the time goes:
time: 19.9 us; the launch traced here: 19.8 us
  Pallas kernels  17.6 us (88%)
  local copies, waits for them, and re-layouts  1.47 us (7%)
  between operations  0.66 us (3%)
    pallas_call x1, Pallas kernels, on_device(): pl.pallas_call(kernel, out_shape=jax.ShapeDtypeStruct((blk, excite.shape[...  17.6 us
    unnamed x1, local copies, waits for them, and re-layouts  1.47 us

commit v1 on v0

--- a/solution.py
+++ b/solution.py
@@ -444,7 +444,7 @@
     dma = pltpu.SemaphoreType.DMA
     return pl.pallas_call(
         kernel,
-        out_shape=jax.ShapeDtypeStruct((blk, excite.shape[0]), jnp.float32),
+        out_shape=pltpu.VMEM((blk, excite.shape[0]), jnp.float32),
         in_specs=[hbm] * 9,
         out_specs=vmem,
         scratch_shapes=[

time: 19.9 us -> 18.4 us (0.925)
  local copies, waits for them, and re-layouts: 1.47 us -> 0.63 us
  Pallas kernels: 17.6 us -> 17 us
    unnamed x1, local copies, waits for them, and re-layouts: 1.47 us -> 0.63 us
    pallas_call x1, Pallas kernels: 17.6 us -> 17 us  [on_device(): pl.pallas_call(kernel, out_shape=pltpu.VMEM((blk, excite.shape[0]), jnp.f...]
where the time goes in v1:
time: 18.4 us; the launch traced here: 18.3 us
  Pallas kernels  17 us (92%)
  between operations  0.66 us (4%)
  local copies, waits for them, and re-layouts  0.63 us (3%)
    pallas_call x1, Pallas kernels, on_device(): pl.pallas_call(kernel, out_shape=pltpu.VMEM((blk, excite.shape[0]), jnp.f...  17 us
    unnamed x1, local copies, waits for them, and re-layouts  0.63 us

profile of v1, /device:TPU:0, one launch (start us, length us, event | category | flops | bytes accessed | tf_op | source)
XLA Modules:
  0.0 18.3 jit_solution(8412257260320619827)
XLA Ops:
  0.7 17.0 %slab.1 = f32[128,128]{1,0:T(8,128)S(1)} custom-call(f32[1]{0:T(128)S(6)} %copy.12.wave_hbm, s32[2,9]{1,0:T(2,128)} %order_hbm.1, f32[6,256]{1,0:T(8,128)} %tgt_hbm.1, f32[3,384]{1,0:T(4,128)} %tnode_hbm.1, bf16[2,192,256]{2,1,0:T(8,128)(2,1)} %tweight_hbm.1, f32[4,16]{1,0:T(4,128)} %geom_hbm.1, bf16[16,128]{1,0:T(8,128)(2,1)} %bitcast.3, ...), custom_call_target="tpu_custom_call" | custom-call | tf_op jit(solution)/shard_map/slab/pallas_call | solution.py:445
  17.7 0.6 %copy.11 = f32[128,128]{1,0:T(8,128)} copy(f32[128,128]{1,0:T(8,128)S(1)} %slab.1) | data formatting | bytes 131072

commit v2 on v1

v2 whole, which is shorter than its diff:
```python
import math

import jax
import jax.numpy as jnp
import numpy as np
from jax import lax
from jax.experimental import pallas as pl
from jax.experimental.pallas import tpu as pltpu
from jax.sharding import PartitionSpec as P

ORDERS = 3
SOFT = 0.05
PI = math.pi
LANES = 128
ROWS = 8
PAIR = 2
MESH = pl.DeviceIdType.MESH
TN = (((0,), (0,)), ((), ()))


def fitted(function, terms):
    nodes = (np.cos((np.arange(terms) + 0.5) * np.pi / terms) + 1.0) / 8.0
    matrix = np.vander(nodes, terms, increasing=True)
    return [float(c) for c in np.linalg.solve(matrix, function(np.sqrt(nodes)))]


COS = fitted(lambda u: np.cos(2.0 * np.pi * u), 6)
SIN = fitted(lambda u: np.sin(2.0 * np.pi * u) / u, 6)


def horner(coefficients, y):
    total = coefficients[-1]
    for c in coefficients[-2::-1]:
        total = total * y + c
    return total


def wave_parts(squared):
    inverse = lax.rsqrt(squared)
    turns = squared * inverse
    u = turns - jnp.round(turns)
    y = u * u
    return inverse, horner(COS, y), u, horner(SIN, y)


def times_i(value):
    half = value.shape[1] // 2
    swapped = pltpu.roll(value, half, 1)
    lane = lax.broadcasted_iota(jnp.int32, value.shape, 1)
    return jnp.where(lane < half, -swapped, swapped)


def split_two(value):
    high = value.astype(jnp.bfloat16)
    return high, (value - high.astype(jnp.float32)).astype(jnp.bfloat16)


def columns_of(rows):
    few, lanes = rows.shape
    pad = jnp.zeros((ROWS - few, lanes), jnp.float32)
    return jnp.concatenate([rows, pad], 0).T


def kernel(
    wave_hbm,
    order_hbm,
    tgt_hbm,
    tnode_hbm,
    tweight_hbm,
    geom_hbm,
    excite_hbm,
    snode_hbm,
    sweight_hbm,
    out_ref,
    small_all,
    bulk_all,
    small_pack,
    bulk_pack,
    tnode_wide,
    tgt_wide,
    tests,
    green_high,
    green_low,
    moment,
    impedance,
    part_send,
    part_recv,
    wave_ref,
    order_ref,
    tgt_ref,
    tnode_ref,
    tweight_ref,
    geom_ref,
    excite_ref,
    snode_ref,
    sweight_ref,
    local,
    own,
    small_send,
    bulk_send,
    small_recv,
    bulk_recv,
    part_sem,
):
    n_row = lax.axis_size("row")
    row = lax.axis_index("row")
    col = lax.axis_index("col")
    home = lax.rem(row, 2)
    place = row // 2
    chips = n_row // 2
    reach = (order_hbm.shape[1] - 1) // 2
    qn = snode_hbm.shape[1]
    tail = qn - LANES
    step_nodes = qn // ORDERS
    per = excite_hbm.shape[0]
    blk, width = out_ref.shape
    near_pairs = moment.shape[0]
    first_pair = jnp.clip(
        (row - reach - col + 1) // 2 // PAIR, 0, chips // PAIR - near_pairs
    )
    mine = home == col

    barrier = pltpu.get_barrier_semaphore()
    upper = row >= chips

    def outward(index, count):
        return jnp.where(upper, index, count - 1 - index)

    @pl.loop(0, n_row)
    def _(index):
        index = outward(index, n_row)
        chip, core = 2 * (index // 2) + col, lax.rem(index, 2)

        @pl.when(jnp.logical_not(jnp.logical_and(chip == row, core == col)))
        def _():
            pl.semaphore_signal(
                barrier, inc=1, device_id={"row": chip, "col": core}, device_id_type=MESH
            )

    @pl.when(jnp.logical_not(mine))
    def _():
        pl.semaphore_signal(barrier, inc=1, device_id={"col": 1 - col}, device_id_type=MESH)

    loads = [
        pltpu.make_async_copy(here, there, local.at[index])
        for index, (here, there) in enumerate(
            (
                (snode_hbm, snode_ref),
                (geom_hbm, geom_ref),
                (excite_hbm, excite_ref),
                (sweight_hbm, sweight_ref),
                (wave_hbm, wave_ref),
                (tnode_hbm, tnode_ref),
                (tgt_hbm, tgt_ref),
                (order_hbm, order_ref),
                (tweight_hbm, tweight_ref),
            )
        )
    ]
    for load in loads:
        load.start()

    lane = lax.broadcasted_iota(jnp.int32, (1, LANES), 1)

    loads[0].wait()
    nodes = snode_ref[...]
    gap = jnp.zeros((nodes.shape[0], LANES - tail), jnp.float32)
    ends = nodes[:, LANES:]
    even, odd = jnp.concatenate([ends, gap], 1), jnp.concatenate([gap, ends], 1)
    ends = jnp.where(lax.rem(place, PAIR) == 0, even, odd)
    small_pack[0:3, :] = jnp.where(col == 0, nodes[:, :LANES], ends)
    loads[1].wait()
    pieces = LANES // (2 * per)
    spread = jnp.concatenate([geom_ref[...]] * (LANES // per), 1)
    begin = (2 * lax.rem(place, pieces) + col) * per
    inside = jnp.logical_and(lane >= begin, lane < begin + per)
    small_pack[3:4, :] = jnp.zeros((1, LANES), jnp.float32)
    small_pack[4:8, :] = jnp.where(inside, spread, 0.0)
    loads[2].wait()
    bulk_pack[0] = excite_ref[...]
    loads[3].wait()
    bulk_pack[1] = sweight_ref[0, :, :LANES]
    bulk_pack[2] = sweight_ref[1, :, :LANES]
    bulk_pack[3] = jnp.concatenate(
        [sweight_ref[part, :, LANES:].astype(jnp.float32) for part in range(2)], 1
    ).astype(jnp.bfloat16)

    @pl.when(mine)
    def _():
        pltpu.make_async_copy(small_pack, small_all.at[place, col], small_recv.at[place]).start()
        pltpu.make_async_copy(bulk_pack, bulk_all.at[place, col], bulk_recv.at[place]).start()

    def small_to(chip):
        return pltpu.make_async_remote_copy(
            src_ref=small_pack,
            dst_ref=small_all.at[place, col],
            send_sem=small_send.at[chip],
            recv_sem=small_recv.at[place],
            device_id={"row": chip, "col": home},
            device_id_type=MESH,
        )

    def bulk_to(chip):
        return pltpu.make_async_remote_copy(
            src_ref=bulk_pack,
            dst_ref=bulk_all.at[place, col],
            send_sem=bulk_send.at[chip],
            recv_sem=bulk_recv.at[place],
            device_id={"row": chip, "col": home},
            device_id_type=MESH,
        )

    def excite_to(chip):
        return pltpu.make_async_remote_copy(
            src_ref=bulk_pack.at[0],
            dst_ref=bulk_all.at[place, col, 0],
            send_sem=bulk_send.at[chip],
            recv_sem=bulk_recv.at[place],
            device_id={"row": chip, "col": home},
            device_id_type=MESH,
        )

    def is_near(chip):
        return jnp.logical_and(chip >= row - reach, chip <= row + reach)

    def for_others(act):
        @pl.loop(0, n_row)
        def _(index):
            chip = outward(index, n_row)

            @pl.when(jnp.logical_not(jnp.logical_and(mine, chip == row)))
            def _():
                act(chip)

    def bulk_act(chip, name):
        near = is_near(chip)

        @pl.when(near)
        def _():
            getattr(bulk_to(chip), name)()

        @pl.when(jnp.logical_not(near))
        def _():
            getattr(excite_to(chip), name)()

    def order_of(block, chip):
        offset = chip - row + reach
        valid = jnp.logical_and(offset >= 0, offset <= 2 * reach)
        value = order_ref[block, jnp.clip(offset, 0, 2 * reach)] * step_nodes
        return jnp.where(valid, value, 0)

    def turns_per_unit():
        return wave_ref[0] * (0.5 / PI)

    def prepare():
        rate = turns_per_unit()
        cols = columns_of(tnode_ref[...])
        origin = cols[0:1]
        cols = (cols - origin) * rate
        for block in range(2):
            for axis in range(3):
                tnode_wide[block, axis] = jnp.broadcast_to(
                    cols[block * qn : (block + 1) * qn, axis : axis + 1], (qn, LANES)
                )
        loads[6].wait()
        cols = columns_of(tgt_ref[...])
        for axis in range(6):
            line = cols[:, axis : axis + 1]
            if axis < 3:
                line = (line - origin[:, axis : axis + 1]) * rate
            tgt_wide[axis] = jnp.broadcast_to(line, (2 * blk, LANES))

        loads[8].wait()
        for block in range(2):
            at = slice(block * blk, (block + 1) * blk)
            tests[block] = jnp.concatenate([tweight_ref[0, :, at], tweight_ref[1, :, at]], 0).T

    def scaled(places):
        rate = turns_per_unit()
        first = tnode_ref[:, 0:1]
        return (places - first) * rate

    def green_of(chunk, places, limits):
        rate = turns_per_unit()
        soft = rate * rate * (SOFT * SOFT)
        places = scaled(places)
        s_x, s_y, s_z = (places[i : i + 1] for i in range(3))

        @pl.loop(0, 2)
        def _(block):
            limit, ahead = limits(block)
            for group in range(ORDERS):
                here = slice(group * step_nodes, (group + 1) * step_nodes)
                live = jnp.logical_and(ahead < limit, limit > group * step_nodes)
                scale = jnp.where(live, rate * (0.25 / PI), 0.0)
                d_x = tnode_wide[block, 0, here] - s_x
                d_y = tnode_wide[block, 1, here] - s_y
                d_z = tnode_wide[block, 2, here] - s_z
                squared = d_x * d_x + d_y * d_y + (d_z * d_z + soft)
                inverse, cosine, u, sine = wave_parts(squared)
                inverse = inverse * scale
                for part, value in enumerate((inverse * cosine, (inverse * u) * sine)):
                    high, low = split_two(value)
                    at = pl.multiple_of((2 * chunk + part) * LANES, LANES)
                    green_high[block, here, pl.ds(at, LANES)] = high
                    green_low[block, here, pl.ds(at, LANES)] = low

    def green_head(pair, slot, places):
        chip = 2 * ((first_pair + pair) * PAIR + slot) + col
        green_of(3 * pair + slot, places, lambda block: (order_of(block, chip), lane))

    def green_tail(pair, places):
        chip = 2 * (first_pair + pair) * PAIR + col

        def limits(block):
            limit = jnp.where(lane < tail, order_of(block, chip), order_of(block, chip + 2))
            return limit, LANES + jnp.where(lane < tail, lane, lane - tail)

        green_of(3 * pair + PAIR, places, limits)

    own_pair = place // PAIR - first_pair
    own_slot = lax.rem(place, PAIR)

    def green_own():
        @pl.when(mine)
        def _():
            green_head(own_pair, own_slot, snode_ref[:, :LANES])

    loads[4].wait()
    loads[5].wait()
    loads[7].wait()

    @pl.when(jnp.logical_not(upper))
    def _():
        prepare()
        green_own()

    pl.semaphore_wait(barrier, n_row)
    for_others(lambda chip: small_to(chip).start())
    for_others(lambda chip: bulk_act(chip, "start"))

    @pl.when(upper)
    def _():
        prepare()
        green_own()

    def wait_small(index):
        pltpu.make_async_copy(small_all.at[index], small_all.at[index], small_recv.at[index]).wait()

    def wait_bulk(index):
        near = is_near(2 * index + col)

        @pl.when(near)
        def _():
            pltpu.make_async_copy(bulk_all.at[index], bulk_all.at[index], bulk_recv.at[index]).wait()

        @pl.when(jnp.logical_not(near))
        def _():
            view = bulk_all.at[index, :, 0]
            pltpu.make_async_copy(view, view, bulk_recv.at[index]).wait()

    @pl.loop(0, near_pairs)
    def _(turn):
        pair = near_pairs - 1 - turn
        base = (first_pair + pair) * PAIR

        @pl.loop(0, PAIR)
        def _(slot):
            slot = PAIR - 1 - slot
            index = base + slot
            chip = 2 * index + col
            wait_small(index)

            @pl.when(jnp.logical_and(is_near(chip), chip != row))
            def _():
                green_head(pair, slot, small_all[index, 0, 0:3])

            @pl.when(jnp.logical_not(is_near(chip)))
            def _():
                at = pl.ds(pl.multiple_of((3 * pair + slot) * 2 * LANES, LANES), 2 * LANES)
                for block in range(2):
                    green_high[block, :, at] = jnp.zeros((qn, 2 * LANES), jnp.bfloat16)
                    green_low[block, :, at] = jnp.zeros((qn, 2 * LANES), jnp.bfloat16)

        green_tail(pair, small_all[base, 1, 0:3] + small_all[base + 1, 1, 0:3])

    for_rest_begin, for_rest_end = PAIR * first_pair, PAIR * (first_pair + near_pairs)

    def for_rest(act):
        if PAIR * near_pairs < chips:

            @pl.loop(0, chips)
            def _(index):
                @pl.when(jnp.logical_or(index < for_rest_begin, index >= for_rest_end))
                def _():
                    act(index)

    for_rest(wait_small)

    rate = turns_per_unit()
    soft = rate * rate * (SOFT * SOFT)

    @pl.loop(0, chips // pieces)
    def _(chunk):
        packed = small_all[pl.ds(chunk * pieces, pieces), :, 4:8, :].reshape(2 * pieces, 4, LANES)
        packed = jnp.sum(packed, 0)
        places = scaled(packed[0:3])
        area = packed[3:4] * (rate * (0.25 / PI))
        at = pl.multiple_of(chunk * 2 * LANES, LANES)
        for part in range(2 * blk // 64):
            here = slice(part * 64, (part + 1) * 64)
            d_x = tgt_wide[0, here] - places[0:1]
            d_y = tgt_wide[1, here] - places[1:2]
            d_z = tgt_wide[2, here] - places[2:3]
            squared = d_x * d_x + d_y * d_y + (d_z * d_z + soft)
            inverse, cosine, u, sine = wave_parts(squared)
            sine = u * sine
            along = (tgt_wide[3, here] * d_x + tgt_wide[4, here] * d_y + tgt_wide[5, here] * d_z) * inverse
            scale = area * inverse
            green_re = scale * cosine
            green_im = scale * sine
            factor_re = 1.0 - along
            factor_im = along * (inverse * (-0.5 / PI))
            impedance[here, pl.ds(at, LANES)] = (green_re * factor_re - green_im * factor_im).astype(jnp.bfloat16)
            impedance[here, pl.ds(at + LANES, LANES)] = (green_re * factor_im + green_im * factor_re).astype(jnp.bfloat16)

    def turned(rows):
        return times_i(rows.astype(jnp.float32)).astype(jnp.bfloat16)

    def put_moment(pair, begin, value):
        both = jnp.concatenate([value, times_i(value)], 0)
        high, low = split_two(both)
        count = value.shape[0]
        for part in range(2):
            at = pl.ds(pl.multiple_of(begin + part * LANES, tail), count)
            here = slice(part * count, (part + 1) * count)
            moment[pair, at, 0:width] = high[here]
            moment[pair, at, width:] = low[here]

    @pl.loop(0, near_pairs)
    def _(turn):
        pair = near_pairs - 1 - turn

        @pl.loop(0, PAIR)
        def _(slot):
            slot = PAIR - 1 - slot
            index = (first_pair + pair) * PAIR + slot
            wait_bulk(index)
            near = is_near(2 * index + col)
            head_at = slot * 2 * LANES
            tail_at = PAIR * 2 * LANES + slot * tail

            @pl.when(near)
            def _():
                rows = bulk_all[index, :, 0].reshape(2 * per, width)
                spun = turned(rows)
                heads = jnp.concatenate([bulk_all[index, half, part] for part in (1, 2) for half in range(2)], 0)
                value = lax.dot_general(
                    heads, jnp.concatenate([rows, spun], 0), TN, preferred_element_type=jnp.float32
                )
                put_moment(pair, head_at, value)
                ends = jnp.concatenate([bulk_all[index, half, 3] for half in range(2)], 0)
                value = lax.dot_general(
                    ends, jnp.concatenate([rows, spun], 1), TN, preferred_element_type=jnp.float32
                )
                put_moment(pair, tail_at, value[:tail, :width] + value[tail:, width:])

            @pl.when(jnp.logical_not(near))
            def _():
                put_moment(pair, head_at, jnp.zeros((LANES, width), jnp.float32))
                put_moment(pair, tail_at, jnp.zeros((tail, width), jnp.float32))

    for_rest(wait_bulk)

    def partial(block):
        def far_step(chunk, total):
            rows = bulk_all[pl.ds(chunk * pieces, pieces), :, 0].reshape(LANES, width)
            at = pl.multiple_of(chunk * 2 * LANES, LANES)
            begin = pl.multiple_of(block * blk, blk)
            return total + jnp.dot(
                impedance[pl.ds(begin, blk), pl.ds(at, 2 * LANES)],
                jnp.concatenate([rows, turned(rows)], 0),
                preferred_element_type=jnp.float32,
            )

        far = lax.fori_loop(0, chips // pieces, far_step, jnp.zeros((blk, width), jnp.float32))
        right = jnp.concatenate([moment[pair] for pair in range(near_pairs)], 0)
        inner = jnp.dot(green_high[block], right, preferred_element_type=jnp.float32)
        inner = inner[:, :width] + inner[:, width:]
        inner = inner + jnp.dot(green_low[block], right[:, :width], preferred_element_type=jnp.float32)
        high, low = split_two(jnp.concatenate([inner, times_i(inner)], 0))
        product = jnp.dot(
            tests[block], jnp.concatenate([high, low], 1), preferred_element_type=jnp.float32
        )
        return far + (product[:, :width] + product[:, width:])

    swap = pltpu.make_async_remote_copy(
        src_ref=part_send,
        dst_ref=part_recv,
        send_sem=part_sem.at[0],
        recv_sem=part_sem.at[1],
        device_id={"col": 1 - col},
        device_id_type=MESH,
    )
    part_send[...] = partial(1 - col)
    swap.start()
    result = partial(col)
    swap.wait_recv()
    out_ref[...] = result + part_recv[...]

    for_others(lambda chip: small_to(chip).wait_send())
    for_others(lambda chip: bulk_act(chip, "wait_send"))
    swap.wait_send()


def on_device(
    wavenumber,
    tgt_geom,
    src_geom,
    excite,
    tgt_nodes,
    src_nodes,
    tgt_weights,
    src_weights,
    near_order,
):
    n_row = lax.axis_size("row")
    chips = n_row // 2
    blk = tgt_geom.shape[1] // 2
    qn = src_nodes.shape[1]
    per, width = src_geom.shape[1], excite.shape[0]
    excite_rows = excite.T
    weight_rows = src_weights.transpose(0, 2, 1)
    near_pairs = min(3, chips // PAIR)
    depth = near_pairs * 3 * 2 * LANES
    hbm = pl.BlockSpec(memory_space=pl.ANY)
    dma = pltpu.SemaphoreType.DMA
    f32, bf16 = jnp.float32, jnp.bfloat16
    return pl.pallas_call(
        kernel,
        out_shape=pltpu.VMEM((blk, width), f32),
        in_specs=[hbm] * 9,
        out_specs=pl.BlockSpec(memory_space=pltpu.VMEM),
        scratch_shapes=[
            pltpu.VMEM((chips, 2, ROWS, LANES), f32),
            pltpu.VMEM((chips, 2, 4, per, LANES), bf16),
            pltpu.VMEM((ROWS, LANES), f32),
            pltpu.VMEM((4, per, LANES), bf16),
            pltpu.VMEM((2, 3, qn, LANES), f32),
            pltpu.VMEM((6, 2 * blk, LANES), f32),
            pltpu.VMEM((2, blk, 2 * qn), bf16),
            pltpu.VMEM((2, qn, depth), bf16),
            pltpu.VMEM((2, qn, depth), bf16),
            pltpu.VMEM((near_pairs, 3 * 2 * LANES, 2 * width), bf16),
            pltpu.VMEM((2 * blk, chips * 4 * per), bf16),
            pltpu.VMEM((blk, width), f32),
            pltpu.VMEM((blk, width), f32),
            pltpu.SMEM(wavenumber.shape, f32),
            pltpu.SMEM(near_order.shape, jnp.int32),
            pltpu.VMEM(tgt_geom.shape, f32),
            pltpu.VMEM(tgt_nodes.shape, f32),
            pltpu.VMEM(tgt_weights.shape, bf16),
            pltpu.VMEM(src_geom.shape, f32),
            pltpu.VMEM(excite_rows.shape, bf16),
            pltpu.VMEM(src_nodes.shape, f32),
            pltpu.VMEM(weight_rows.shape, bf16),
            dma((9,)),
            dma((2,)),
            dma((n_row,)),
            dma((n_row,)),
            dma((chips,)),
            dma((chips,)),
            dma((2,)),
        ],
        compiler_params=pltpu.CompilerParams(collective_id=0, has_side_effects=True),
        name="slab",
    )(
        wavenumber,
        near_order,
        tgt_geom,
        tgt_nodes,
        tgt_weights,
        src_geom,
        excite_rows,
        src_nodes,
        weight_rows,
    )


def solution(mesh):
    return jax.shard_map(
        on_device,
        mesh=mesh,
        in_specs=(
            P("groups"),
            P(None, ("groups", "row")),
            P(None, ("groups", "row", "col")),
            P(None, ("groups", "row", "col")),
            P(None, ("groups", "row")),
            P(None, ("groups", "row")),
            P(None, None, ("groups", "row")),
            P(None, None, ("groups", "row", "col")),
            P(("groups", "row"), None),
        ),
        out_specs=P(("groups", "row", "col"), None),
        check_vma=False,
    )
```

time: 18.4 us -> 15.3 us (0.83)
  Pallas kernels: 17 us -> 13.8 us
    pallas_call x1, Pallas kernels: 17 us -> 13.8 us  [on_device(): pl.pallas_call(kernel, out_shape=pltpu.VMEM((blk, width), f32), in_specs=...]
where the time goes in v2:
time: 15.3 us; the launch traced here: 15.1 us
  Pallas kernels  13.8 us (90%)
  between operations  0.66 us (4%)
  local copies, waits for them, and re-layouts  0.63 us (4%)
    pallas_call x1, Pallas kernels, on_device(): pl.pallas_call(kernel, out_shape=pltpu.VMEM((blk, width), f32), in_specs=...  13.8 us
    unnamed x1, local copies, waits for them, and re-layouts  0.63 us

profile of v2, /device:TPU:0, one launch (start us, length us, event | category | flops | bytes accessed | tf_op | source)
XLA Modules:
  0.0 15.1 jit_solution(9444030985906619244)
XLA Ops:
  0.7 13.8 %slab.1 = f32[128,128]{1,0:T(8,128)S(1)} custom-call(f32[1]{0:T(128)S(6)} %copy.12.wave_hbm, s32[2,9]{1,0:T(2,128)} %order_hbm.1, f32[6,256]{1,0:T(8,128)} %tgt_hbm.1, f32[3,384]{1,0:T(4,128)} %tnode_hbm.1, bf16[2,192,256]{2,1,0:T(8,128)(2,1)} %tweight_hbm.1, f32[4,16]{1,0:T(4,128)} %geom_hbm.1, bf16[16,128]{1,0:T(8,128)(2,1)} %bitcast.3, ...), custom_call_target="tpu_custom_call" | custom-call | tf_op jit(solution)/shard_map/slab/pallas_call | solution.py:539
  14.5 0.6 %copy.11 = f32[128,128]{1,0:T(8,128)} copy(f32[128,128]{1,0:T(8,128)S(1)} %slab.1) | data formatting | bytes 131072

commit v3 on v2

v3 whole, which is shorter than its diff:
```python
import math

import jax
import jax.numpy as jnp
import numpy as np
from jax import lax
from jax.experimental import pallas as pl
from jax.experimental.pallas import tpu as pltpu
from jax.sharding import PartitionSpec as P

ORDERS = 3
SOFT = 0.05
PI = math.pi
LANES = 128
ROWS = 8
MESH = pl.DeviceIdType.MESH
TN = (((0,), (0,)), ((), ()))


def fitted(function, terms):
    nodes = (np.cos((np.arange(terms) + 0.5) * np.pi / terms) + 1.0) / 8.0
    matrix = np.vander(nodes, terms, increasing=True)
    return [float(c) for c in np.linalg.solve(matrix, function(np.sqrt(nodes)))]


COS = fitted(lambda u: np.cos(2.0 * np.pi * u), 6)
SIN = fitted(lambda u: np.sin(2.0 * np.pi * u) / u, 6)


def horner(coefficients, y):
    total = coefficients[-1]
    for c in coefficients[-2::-1]:
        total = total * y + c
    return total


def wave_parts(squared):
    inverse = lax.rsqrt(squared)
    turns = squared * inverse
    u = turns - jnp.round(turns)
    y = u * u
    return inverse, horner(COS, y), u, horner(SIN, y)


def plus_i(first, second):
    half = second.shape[1] // 2
    swapped = pltpu.roll(second, half, 1)
    lane = lax.broadcasted_iota(jnp.int32, second.shape, 1)
    return first + jnp.where(lane < half, -swapped, swapped)


def split_two(value):
    high = value.astype(jnp.bfloat16)
    return high, (value - high.astype(jnp.float32)).astype(jnp.bfloat16)


def columns_of(rows):
    few, lanes = rows.shape
    pad = jnp.zeros((ROWS - few, lanes), jnp.float32)
    return jnp.concatenate([rows, pad], 0).T


def kernel(
    wave_hbm,
    order_hbm,
    tgt_hbm,
    tnode_hbm,
    tweight_hbm,
    geom_hbm,
    excite_hbm,
    snode_hbm,
    sweight_hbm,
    out_ref,
    node_all,
    bulk_all,
    bulk_pack,
    tnode_wide,
    tgt_wide,
    tests,
    green_high,
    green_low,
    moment,
    impedance,
    far_send,
    far_recv,
    far_own,
    wave_ref,
    order_ref,
    tgt_ref,
    tnode_ref,
    tweight_ref,
    geom_ref,
    excite_ref,
    snode_ref,
    sweight_ref,
    local,
    node_send,
    node_recv,
    bulk_send,
    bulk_recv,
    moment_send,
    moment_recv,
    far_sem,
):
    n_row = lax.axis_size("row")
    row = lax.axis_index("row")
    col = lax.axis_index("col")
    home = lax.rem(row, 2)
    place = row // 2
    chips = n_row // 2
    band = node_all.shape[0]
    reach = (band - 1) // 2
    qn = snode_hbm.shape[1]
    tail = qn - LANES
    step_nodes = qn // ORDERS
    per = excite_hbm.shape[0]
    blk, width = out_ref.shape
    near_pairs = moment.shape[0]
    first_pair = jnp.clip((row - reach + band - 1) // 2 - (band - 1) // 2, 0, chips - near_pairs)
    mine = home == col
    upper = row >= chips
    lane = lax.broadcasted_iota(jnp.int32, (1, LANES), 1)

    def outward(index, count):
        return jnp.where(upper, index, count - 1 - index)

    barrier = pltpu.get_barrier_semaphore()

    def greet(chip, core):
        pl.semaphore_signal(
            barrier, inc=1, device_id={"row": chip, "col": core}, device_id_type=MESH
        )

    @pl.loop(0, n_row)
    def _(index):
        chip = outward(index, n_row)

        @pl.when(chip != row)
        def _():
            greet(chip, col)

        @pl.when(jnp.logical_or(lax.rem(chip, 2) == col, chip == row))
        def _():
            greet(chip, 1 - col)

    loads = [
        pltpu.make_async_copy(here, there, local.at[index])
        for index, (here, there) in enumerate(
            (
                (geom_hbm, geom_ref),
                (excite_hbm, excite_ref),
                (snode_hbm, snode_ref),
                (sweight_hbm, sweight_ref),
                (wave_hbm, wave_ref),
                (tnode_hbm, tnode_ref),
                (tgt_hbm, tgt_ref),
                (order_hbm, order_ref),
                (tweight_hbm, tweight_ref),
            )
        )
    ]
    for load in loads:
        load.start()

    loads[0].wait()
    pieces = LANES // (2 * per)
    spread = jnp.concatenate([geom_ref[...]] * (LANES // per), 1)
    begin = (2 * lax.rem(place, pieces) + col) * per
    inside = jnp.logical_and(lane >= begin, lane < begin + per)
    spread = jnp.where(inside, spread, 0.0)
    first = spread.astype(jnp.bfloat16).astype(jnp.float32)
    second = (spread - first).astype(jnp.bfloat16).astype(jnp.float32)
    third = (spread - first) - second
    rest = jnp.zeros((per - 12, LANES), jnp.float32)
    bulk_pack[1] = jnp.concatenate([first, second, third, rest], 0).astype(jnp.bfloat16)
    loads[1].wait()
    bulk_pack[0] = excite_ref[...]
    loads[2].wait()
    nodes = snode_ref[...]
    gap = jnp.zeros((nodes.shape[0], LANES - tail), jnp.float32)
    even = lax.rem(row, 2) == 0
    node_all[reach, 0:3] = jnp.where(even, nodes[:, :LANES], nodes[:, qn - LANES :])
    node_all[reach, 4:7] = jnp.where(
        even,
        jnp.concatenate([nodes[:, LANES:], gap], 1),
        jnp.concatenate([gap, nodes[:, :tail]], 1),
    )
    node_all[reach, 3:4] = jnp.zeros((1, LANES), jnp.float32)
    node_all[reach, 7:8] = jnp.zeros((1, LANES), jnp.float32)
    loads[3].wait()
    bulk_pack[2] = sweight_ref[0, :, :LANES]
    bulk_pack[3] = jnp.concatenate(
        [sweight_ref[0, :, LANES:].astype(jnp.float32), sweight_ref[1, :, :tail].astype(jnp.float32)], 1
    ).astype(jnp.bfloat16)
    bulk_pack[4] = sweight_ref[1, :, tail:]

    @pl.when(mine)
    def _():
        pltpu.make_async_copy(bulk_pack, bulk_all.at[place, col], bulk_recv.at[place]).start()

    def node_to(chip):
        slot = row - chip + reach
        return pltpu.make_async_remote_copy(
            src_ref=node_all.at[reach],
            dst_ref=node_all.at[slot],
            send_sem=node_send.at[slot],
            recv_sem=node_recv.at[slot],
            device_id={"row": chip},
            device_id_type=MESH,
        )

    def bulk_to(chip, planes):
        return pltpu.make_async_remote_copy(
            src_ref=bulk_pack.at[pl.ds(0, planes)],
            dst_ref=bulk_all.at[place, col, pl.ds(0, planes)],
            send_sem=bulk_send.at[chip],
            recv_sem=bulk_recv.at[place],
            device_id={"row": chip, "col": home},
            device_id_type=MESH,
        )

    def is_near(chip):
        return jnp.logical_and(chip >= row - reach, chip <= row + reach)

    def for_sends(name):
        @pl.loop(0, n_row)
        def _(index):
            chip = outward(index, n_row)
            near = is_near(chip)

            @pl.when(jnp.logical_and(near, chip != row))
            def _():
                getattr(node_to(chip), name)()

            @pl.when(jnp.logical_and(near, jnp.logical_not(jnp.logical_and(mine, chip == row))))
            def _():
                getattr(bulk_to(chip, 5), name)()

            @pl.when(jnp.logical_not(near))
            def _():
                getattr(bulk_to(chip, 2), name)()

    def order_of(chip):
        offset = jnp.clip(chip - row + reach, 0, 2 * reach)
        return jnp.where(is_near(chip), order_ref[col, offset] * step_nodes, 0)

    def turns_per_unit():
        return wave_ref[0] * (0.5 / PI)

    def scaled(places):
        return (places - tnode_ref[:, 0:1]) * turns_per_unit()

    def prepare():
        rate = turns_per_unit()
        begin = pl.multiple_of(col * blk, blk)
        cols = columns_of(tnode_ref[...])
        origin = cols[0:1]
        cols = jnp.where(col == 0, cols[:qn], cols[qn:])
        cols = (cols - origin) * rate
        for axis in range(3):
            tnode_wide[axis] = jnp.broadcast_to(cols[:, axis : axis + 1], (qn, LANES))
        loads[6].wait()
        cols = columns_of(tgt_ref[...])
        for axis in range(6):
            line = cols[:, axis : axis + 1]
            if axis < 3:
                line = (line - origin[:, axis : axis + 1]) * rate
            tgt_wide[axis] = jnp.broadcast_to(line, (2 * blk, LANES))
        loads[8].wait()
        for part in range(2):
            tests[part * blk : (part + 1) * blk] = tweight_ref[part, :, pl.ds(begin, blk)].T
        for pair in range(near_pairs):
            for core in range(2):

                @pl.when(jnp.logical_not(is_near(2 * (first_pair + pair) + core)))
                def _():
                    moment[pair, core * qn : (core + 1) * qn] = jnp.zeros((qn, 2 * width), jnp.bfloat16)
                    at = (3 * pair + 2 * core) * LANES
                    green_high[:, at : at + LANES] = jnp.zeros((2 * qn, LANES), jnp.bfloat16)
                    green_low[:, at : at + LANES] = jnp.zeros((2 * qn, LANES), jnp.bfloat16)

    def green_of(chunk, places, limit, ahead):
        rate = turns_per_unit()
        soft = rate * rate * (SOFT * SOFT)
        places = scaled(places)
        s_x, s_y, s_z = (places[i : i + 1] for i in range(3))
        at = pl.ds(pl.multiple_of(chunk * LANES, LANES), LANES)
        for group in range(ORDERS):
            here = slice(group * step_nodes, (group + 1) * step_nodes)
            live = jnp.logical_and(ahead < limit, limit > group * step_nodes)
            scale = jnp.where(live, rate * (0.25 / PI), 0.0)
            d_x = tnode_wide[0, here] - s_x
            d_y = tnode_wide[1, here] - s_y
            d_z = tnode_wide[2, here] - s_z
            squared = d_x * d_x + d_y * d_y + (d_z * d_z + soft)
            inverse, cosine, u, sine = wave_parts(squared)
            inverse = inverse * scale
            for part, value in enumerate((inverse * cosine, (inverse * u) * sine)):
                high, low = split_two(value)
                to = slice(part * qn + group * step_nodes, part * qn + (group + 1) * step_nodes)
                green_high[to, at] = high
                green_low[to, at] = low

    def green_head(pair, core, places):
        limit = order_of(2 * (first_pair + pair) + core)
        green_of(3 * pair + 2 * core, places, limit, lane + core * tail)

    def slot_of(chip):
        return jnp.clip(chip - row + reach, 0, band - 1)

    def green_middle(pair):
        chip = 2 * (first_pair + pair)
        places = jnp.zeros((3, LANES), jnp.float32)
        for core in range(2):
            value = node_all[slot_of(chip + core), 4:7]
            places = places + jnp.where(is_near(chip + core), value, 0.0)
        limit = jnp.where(lane < tail, order_of(chip), order_of(chip + 1))
        green_of(3 * pair + 1, places, limit, jnp.where(lane < tail, lane + LANES, lane - tail))

    def green_own():
        green_head(place - first_pair, home, node_all[reach, 0:3])

    def green_pair(pair):
        @pl.loop(0, 2)
        def _(core):
            chip = 2 * (first_pair + pair) + core
            slot = slot_of(chip)

            @pl.when(jnp.logical_and(is_near(chip), chip != row))
            def _():
                view = node_all.at[slot]
                pltpu.make_async_copy(view, view, node_recv.at[slot]).wait()
                green_head(pair, core, node_all[slot, 0:3])

        green_middle(pair)

    def pair_live(pair):
        chip = 2 * (first_pair + pair)
        return jnp.logical_or(is_near(chip), is_near(chip + 1))

    def green_some(begin, end):
        @pl.loop(begin, end)
        def _(turn):
            pair = near_pairs - 1 - turn

            @pl.when(pair_live(pair))
            def _():
                green_pair(pair)

            @pl.when(jnp.logical_not(pair_live(pair)))
            def _():
                at = pl.ds(pl.multiple_of((3 * pair + 1) * LANES, LANES), LANES)
                green_high[:, at] = jnp.zeros((2 * qn, LANES), jnp.bfloat16)
                green_low[:, at] = jnp.zeros((2 * qn, LANES), jnp.bfloat16)

    loads[4].wait()
    loads[5].wait()
    loads[7].wait()

    @pl.when(jnp.logical_not(upper))
    def _():
        prepare()
        green_own()

    pl.semaphore_wait(barrier, jnp.where(mine, n_row, 2 * n_row - 1))
    for_sends("start")

    @pl.when(upper)
    def _():
        prepare()
        green_own()

    green_some(0, near_pairs - 1)

    def wait_bulk(index):
        near = is_near(2 * index + col)
        for planes, go in ((5, near), (2, jnp.logical_not(near))):

            @pl.when(go)
            def _():
                view = bulk_all.at[index, :, pl.ds(0, planes)]
                pltpu.make_async_copy(view, view, bulk_recv.at[index]).wait()

    @pl.loop(0, near_pairs)
    def _(turn):
        wait_bulk(first_pair + near_pairs - 1 - turn)

    for pair in range(near_pairs):
        index = first_pair + pair
        rows = bulk_all[index, :, 0].reshape(2 * per, width)
        weights = jnp.concatenate(
            [bulk_all[index, :, 2 + part].reshape(2 * per, LANES) for part in range(3)], 1
        )
        both = lax.dot_general(weights, rows, TN, preferred_element_type=jnp.float32)
        value = plus_i(both[:qn], both[qn:])
        value = jnp.where(is_near(2 * index + col), value, 0.0)
        high, low = split_two(value)
        at = pl.ds(pl.multiple_of(col * qn, tail), qn)
        moment[pair, at, 0:width] = high
        moment[pair, at, width:] = low

    def moment_to(pair, core):
        view = moment.at[pair, pl.ds(pl.multiple_of(core * qn, tail), qn)]
        return pltpu.make_async_remote_copy(
            src_ref=view,
            dst_ref=view,
            send_sem=moment_send.at[pair],
            recv_sem=moment_recv.at[pair],
            device_id={"col": 1 - col},
            device_id_type=MESH,
        )

    def for_moments(core, name):
        @pl.loop(0, near_pairs)
        def _(pair):
            @pl.when(is_near(2 * (first_pair + pair) + core))
            def _():
                getattr(moment_to(pair, core), name)()

    for_moments(col, "start")

    if near_pairs < chips:

        @pl.loop(0, chips)
        def _(index):
            @pl.when(jnp.logical_or(index < first_pair, index >= first_pair + near_pairs))
            def _():
                wait_bulk(index)

    rate = turns_per_unit()
    soft = rate * rate * (SOFT * SOFT)

    @pl.loop(0, chips // pieces)
    def _(chunk):
        packed = bulk_all[pl.ds(chunk * pieces, pieces), :, 1].reshape(2 * pieces, per, LANES)
        packed = jnp.sum(packed.astype(jnp.float32), 0)
        packed = packed[0:4] + packed[4:8] + packed[8:12]
        places = scaled(packed[0:3])
        area = packed[3:4] * (rate * (0.25 / PI))
        rows = bulk_all[pl.ds(chunk * pieces, pieces), :, 0].reshape(LANES, width)

        def impedance_of(block, total):
            begin = pl.multiple_of(block * blk, blk)
            for part in range(2):
                here = pl.ds(begin + part * (blk // 2), blk // 2)
                d_x = tgt_wide[0, here] - places[0:1]
                d_y = tgt_wide[1, here] - places[1:2]
                d_z = tgt_wide[2, here] - places[2:3]
                squared = d_x * d_x + d_y * d_y + (d_z * d_z + soft)
                inverse, cosine, u, sine = wave_parts(squared)
                sine = u * sine
                along = tgt_wide[3, here] * d_x + tgt_wide[4, here] * d_y + tgt_wide[5, here] * d_z
                along = along * inverse
                scale = area * inverse
                green_re = scale * cosine
                green_im = scale * sine
                factor_re = 1.0 - along
                factor_im = along * (inverse * (-0.5 / PI))
                at = part * (blk // 2)
                impedance[at : at + blk // 2] = (
                    green_re * factor_re - green_im * factor_im
                ).astype(jnp.bfloat16)
                impedance[blk + at : blk + at + blk // 2] = (
                    green_re * factor_im + green_im * factor_re
                ).astype(jnp.bfloat16)
            both = jnp.dot(impedance[...], rows, preferred_element_type=jnp.float32)
            fresh = plus_i(both[:blk], both[blk:])
            total[...] = jnp.where(chunk == 0, fresh, total[...] + fresh)

        impedance_of(1 - col, far_send)
        impedance_of(col, far_own)

    swap = pltpu.make_async_remote_copy(
        src_ref=far_send,
        dst_ref=far_recv,
        send_sem=far_sem.at[0],
        recv_sem=far_sem.at[1],
        device_id={"col": 1 - col},
        device_id_type=MESH,
    )
    swap.start()

    green_some(near_pairs - 1, near_pairs)

    for_moments(1 - col, "wait_recv")
    right = moment[...].reshape(near_pairs * 2 * qn, 2 * width)
    both = jnp.dot(green_high[...], right, preferred_element_type=jnp.float32)
    both = both[:, :width] + both[:, width:]
    both = both + jnp.dot(green_low[...], right[:, :width], preferred_element_type=jnp.float32)
    high, low = split_two(plus_i(both[:qn], both[qn:]))
    both = jnp.dot(tests[...], jnp.concatenate([high, low], 1), preferred_element_type=jnp.float32)
    both = both[:, :width] + both[:, width:]
    near = plus_i(both[:blk], both[blk:])
    swap.wait_recv()
    out_ref[...] = (far_own[...] + far_recv[...]) + near

    for_sends("wait_send")
    for_moments(col, "wait_send")
    swap.wait_send()


def on_device(
    wavenumber,
    tgt_geom,
    src_geom,
    excite,
    tgt_nodes,
    src_nodes,
    tgt_weights,
    src_weights,
    near_order,
):
    n_row = lax.axis_size("row")
    chips = n_row // 2
    band = near_order.shape[1]
    blk = tgt_geom.shape[1] // 2
    qn = src_nodes.shape[1]
    per, width = src_geom.shape[1], excite.shape[0]
    excite_rows = excite.T
    weight_rows = src_weights.transpose(0, 2, 1)
    near_pairs = min(band // 2 + 1, chips)
    depth = near_pairs * 2 * qn
    hbm = pl.BlockSpec(memory_space=pl.ANY)
    dma = pltpu.SemaphoreType.DMA
    f32, bf16 = jnp.float32, jnp.bfloat16
    return pl.pallas_call(
        kernel,
        out_shape=pltpu.VMEM((blk, width), f32),
        in_specs=[hbm] * 9,
        out_specs=pl.BlockSpec(memory_space=pltpu.VMEM),
        scratch_shapes=[
            pltpu.VMEM((band, ROWS, LANES), f32),
            pltpu.VMEM((chips, 2, 5, per, LANES), bf16),
            pltpu.VMEM((5, per, LANES), bf16),
            pltpu.VMEM((3, qn, LANES), f32),
            pltpu.VMEM((6, 2 * blk, LANES), f32),
            pltpu.VMEM((2 * blk, qn), bf16),
            pltpu.VMEM((2 * qn, depth), bf16),
            pltpu.VMEM((2 * qn, depth), bf16),
            pltpu.VMEM((near_pairs, 2 * qn, 2 * width), bf16),
            pltpu.VMEM((2 * blk, LANES), bf16),
            pltpu.VMEM((blk, width), f32),
            pltpu.VMEM((blk, width), f32),
            pltpu.VMEM((blk, width), f32),
            pltpu.SMEM(wavenumber.shape, f32),
            pltpu.SMEM(near_order.shape, jnp.int32),
            pltpu.VMEM(tgt_geom.shape, f32),
            pltpu.VMEM(tgt_nodes.shape, f32),
            pltpu.VMEM(tgt_weights.shape, bf16),
            pltpu.VMEM(src_geom.shape, f32),
            pltpu.VMEM(excite_rows.shape, bf16),
            pltpu.VMEM(src_nodes.shape, f32),
            pltpu.VMEM(weight_rows.shape, bf16),
            dma((9,)),
            dma((band,)),
            dma((band,)),
            dma((n_row,)),
            dma((chips,)),
            dma((near_pairs,)),
            dma((near_pairs,)),
            dma((2,)),
        ],
        compiler_params=pltpu.CompilerParams(collective_id=0, has_side_effects=True),
        name="slab",
    )(
        wavenumber,
        near_order,
        tgt_geom,
        tgt_nodes,
        tgt_weights,
        src_geom,
        excite_rows,
        src_nodes,
        weight_rows,
    )


def solution(mesh):
    return jax.shard_map(
        on_device,
        mesh=mesh,
        in_specs=(
            P("groups"),
            P(None, ("groups", "row")),
            P(None, ("groups", "row", "col")),
            P(None, ("groups", "row", "col")),
            P(None, ("groups", "row")),
            P(None, ("groups", "row")),
            P(None, None, ("groups", "row")),
            P(None, None, ("groups", "row", "col")),
            P(("groups", "row"), None),
        ),
        out_specs=P(("groups", "row", "col"), None),
        check_vma=False,
    )
```

time: 15.3 us -> 15.3 us (level)
  the two profiles are of different devices: /device:TPU:0 before, /device:TPU:3 now
where the time goes in v3:
time: 15.3 us; the launch traced here: 15.1 us
  Pallas kernels  13.8 us (90%)
  between operations  0.66 us (4%)
  local copies, waits for them, and re-layouts  0.63 us (4%)
    pallas_call x1, Pallas kernels, on_device(): pl.pallas_call(kernel, out_shape=pltpu.VMEM((blk, width), f32), in_specs=...  13.8 us
    unnamed x1, local copies, waits for them, and re-layouts  0.63 us

profile of v3, /device:TPU:3, one launch (start us, length us, event | category | flops | bytes accessed | tf_op | source)
XLA Modules:
  0.0 15.1 jit_solution(13992896290590406290)
XLA Ops:
  0.7 13.8 %slab.1 = f32[128,128]{1,0:T(8,128)S(1)} custom-call(f32[1]{0:T(128)S(6)} %copy.12.wave_hbm, s32[2,9]{1,0:T(2,128)} %order_hbm.1, f32[6,256]{1,0:T(8,128)} %tgt_hbm.1, f32[3,384]{1,0:T(4,128)} %tnode_hbm.1, bf16[2,192,256]{2,1,0:T(8,128)(2,1)} %tweight_hbm.1, f32[4,16]{1,0:T(4,128)} %geom_hbm.1, bf16[16,128]{1,0:T(8,128)(2,1)} %bitcast.3, ...), custom_call_target="tpu_custom_call" | custom-call | tf_op jit(solution)/shard_map/slab/pallas_call | solution.py:526
  14.5 0.6 %copy.11 = f32[128,128]{1,0:T(8,128)} copy(f32[128,128]{1,0:T(8,128)S(1)} %slab.1) | data formatting | bytes 131072

commit v4 on v2

v4 whole, which is shorter than its diff:
```python
import math

import jax
import jax.numpy as jnp
import numpy as np
from jax import lax
from jax.experimental import pallas as pl
from jax.experimental.pallas import tpu as pltpu
from jax.sharding import PartitionSpec as P

ORDERS = 3
SOFT = 0.05
PI = math.pi
LANES = 128
ROWS = 8
MESH = pl.DeviceIdType.MESH
TN = (((0,), (0,)), ((), ()))


def fitted(function, terms):
    nodes = (np.cos((np.arange(terms) + 0.5) * np.pi / terms) + 1.0) / 8.0
    matrix = np.vander(nodes, terms, increasing=True)
    return [float(c) for c in np.linalg.solve(matrix, function(np.sqrt(nodes)))]


COS = fitted(lambda u: np.cos(2.0 * np.pi * u), 6)
SIN = fitted(lambda u: np.sin(2.0 * np.pi * u) / u, 6)


def horner(coefficients, y):
    total = coefficients[-1]
    for c in coefficients[-2::-1]:
        total = total * y + c
    return total


def wave_parts(squared):
    inverse = lax.rsqrt(squared)
    turns = squared * inverse
    u = turns - jnp.round(turns)
    y = u * u
    return inverse, horner(COS, y), u, horner(SIN, y)


def plus_i(first, second):
    half = second.shape[1] // 2
    swapped = pltpu.roll(second, half, 1)
    lane = lax.broadcasted_iota(jnp.int32, second.shape, 1)
    return first + jnp.where(lane < half, -swapped, swapped)


def split_two(value):
    high = value.astype(jnp.bfloat16)
    return high, (value - high.astype(jnp.float32)).astype(jnp.bfloat16)


def columns_of(rows):
    few, lanes = rows.shape
    pad = jnp.zeros((ROWS - few, lanes), jnp.float32)
    return jnp.concatenate([rows, pad], 0).T


def kernel(
    wave_hbm,
    order_hbm,
    tgt_hbm,
    tnode_hbm,
    tweight_hbm,
    geom_hbm,
    excite_hbm,
    snode_hbm,
    sweight_hbm,
    out_ref,
    small_all,
    bulk_all,
    small_pack,
    bulk_pack,
    tnode_wide,
    tgt_wide,
    origin,
    scale_all,
    tests,
    green_high,
    green_low,
    moment,
    impedance,
    part_send,
    part_recv,
    wave_ref,
    order_ref,
    tgt_ref,
    tnode_ref,
    tweight_ref,
    geom_ref,
    excite_ref,
    snode_ref,
    sweight_ref,
    local,
    small_send,
    bulk_send,
    small_recv,
    bulk_recv,
    part_sem,
):
    n_row = lax.axis_size("row")
    row = lax.axis_index("row")
    col = lax.axis_index("col")
    home = lax.rem(row, 2)
    place = row // 2
    chips = n_row // 2
    reach = (order_hbm.shape[1] - 1) // 2
    qn = snode_hbm.shape[1]
    tail = qn - LANES
    step_nodes = qn // ORDERS
    per = excite_hbm.shape[0]
    blk, width = out_ref.shape
    near_pairs = moment.shape[0]
    first_pair = jnp.clip(
        (row - reach - col + 1 + 4 * reach) // 4 - reach, 0, chips // 2 - near_pairs
    )
    mine = home == col
    upper = row >= chips
    lane = lax.broadcasted_iota(jnp.int32, (1, LANES), 1)

    def outward(index, count):
        return jnp.where(upper, index, count - 1 - index)

    barrier = pltpu.get_barrier_semaphore()

    @pl.loop(0, n_row)
    def _(index):
        index = outward(index, n_row)
        chip, core = 2 * (index // 2) + col, lax.rem(index, 2)

        @pl.when(jnp.logical_not(jnp.logical_and(chip == row, core == col)))
        def _():
            pl.semaphore_signal(
                barrier, inc=1, device_id={"row": chip, "col": core}, device_id_type=MESH
            )

    @pl.when(jnp.logical_not(mine))
    def _():
        pl.semaphore_signal(barrier, inc=1, device_id={"col": 1 - col}, device_id_type=MESH)

    loads = [
        pltpu.make_async_copy(here, there, local.at[index])
        for index, (here, there) in enumerate(
            (
                (snode_hbm, snode_ref),
                (geom_hbm, geom_ref),
                (excite_hbm, excite_ref),
                (sweight_hbm, sweight_ref),
                (wave_hbm, wave_ref),
                (tnode_hbm, tnode_ref),
                (tgt_hbm, tgt_ref),
                (order_hbm, order_ref),
                (tweight_hbm, tweight_ref),
            )
        )
    ]
    for load in loads:
        load.start()

    def heads_of(nodes):
        return jnp.where(lax.rem(place, 2) == 0, nodes[:, :LANES], nodes[:, tail:])

    loads[0].wait()
    nodes = snode_ref[...]
    gap = jnp.zeros((nodes.shape[0], LANES - tail), jnp.float32)
    ends = jnp.where(
        lax.rem(place, 2) == 0,
        jnp.concatenate([nodes[:, LANES:], gap], 1),
        jnp.concatenate([gap, nodes[:, :tail]], 1),
    )
    small_pack[0:3, :] = jnp.where(col == 0, heads_of(nodes), ends)
    loads[1].wait()
    pieces = LANES // (2 * per)
    spread = jnp.concatenate([geom_ref[...]] * (LANES // per), 1)
    begin = (2 * lax.rem(place, pieces) + col) * per
    inside = jnp.logical_and(lane >= begin, lane < begin + per)
    small_pack[3:4, :] = jnp.zeros((1, LANES), jnp.float32)
    small_pack[4:8, :] = jnp.where(inside, spread, 0.0)

    @pl.when(mine)
    def _():
        pltpu.make_async_copy(small_pack, small_all.at[place, col], small_recv.at[place]).start()

    def pack_bulk():
        loads[2].wait()
        bulk_pack[0] = excite_ref[...]
        loads[3].wait()
        bulk_pack[1] = sweight_ref[0, :, :LANES]
        bulk_pack[2] = jnp.concatenate(
            [sweight_ref[0, :, LANES:].astype(jnp.float32), sweight_ref[1, :, :tail].astype(jnp.float32)], 1
        ).astype(jnp.bfloat16)
        bulk_pack[3] = sweight_ref[1, :, tail:]

        @pl.when(mine)
        def _():
            pltpu.make_async_copy(bulk_pack, bulk_all.at[place, col], bulk_recv.at[place]).start()

    def small_to(chip):
        return pltpu.make_async_remote_copy(
            src_ref=small_pack,
            dst_ref=small_all.at[place, col],
            send_sem=small_send.at[chip],
            recv_sem=small_recv.at[place],
            device_id={"row": chip, "col": home},
            device_id_type=MESH,
        )

    def bulk_to(chip, planes):
        return pltpu.make_async_remote_copy(
            src_ref=bulk_pack.at[pl.ds(0, planes)],
            dst_ref=bulk_all.at[place, col, pl.ds(0, planes)],
            send_sem=bulk_send.at[chip],
            recv_sem=bulk_recv.at[place],
            device_id={"row": chip, "col": home},
            device_id_type=MESH,
        )

    def is_near(chip):
        return jnp.logical_and(chip >= row - reach, chip <= row + reach)

    def for_others(act, begin, end):
        @pl.loop(begin, end)
        def _(chip):
            @pl.when(jnp.logical_not(jnp.logical_and(mine, chip == row)))
            def _():
                act(chip)

    def small_act(name):
        return lambda chip: getattr(small_to(chip), name)()

    def bulk_act(name):
        def act(chip):
            near = is_near(chip)

            @pl.when(near)
            def _():
                getattr(bulk_to(chip, 4), name)()

            @pl.when(jnp.logical_not(near))
            def _():
                getattr(bulk_to(chip, 1), name)()

        return act

    def order_of(block, chip):
        offset = jnp.clip(chip - row + reach, 0, 2 * reach)
        return jnp.where(is_near(chip), order_ref[block, offset] * step_nodes, 0)

    def chip_of(pair, slot):
        return 4 * (first_pair + pair) + 2 * slot + col

    def prepare():
        loads[4].wait()
        loads[5].wait()
        loads[7].wait()
        rate = wave_ref[0] * (0.5 / PI)
        origin[0:3] = jnp.broadcast_to(tnode_ref[:, 0:1], (3, LANES))
        cols = columns_of(tnode_ref[...])
        first = cols[0:1]
        cols = (cols - first) * rate
        for block in range(2):
            for axis in range(3):
                tnode_wide[block, axis] = jnp.broadcast_to(
                    cols[block * qn : (block + 1) * qn, axis : axis + 1], (qn, LANES)
                )

        @pl.loop(0, near_pairs)
        def _(pair):
            for block in range(2):
                even, odd = (order_of(block, chip_of(pair, slot)) for slot in range(2))
                middle = jnp.where(lane < tail, even, odd)
                for part, (limit, ahead) in enumerate(
                    (
                        (even, lane),
                        (middle, jnp.where(lane < tail, lane + LANES, lane - tail)),
                        (odd, lane + tail),
                    )
                ):
                    for group in range(ORDERS):
                        live = jnp.logical_and(ahead < limit, limit > group * step_nodes)
                        value = jnp.where(live, rate * (0.25 / PI), 0.0)
                        at = (3 * pair + part) * 2 + block
                        scale_all[at, group] = jnp.broadcast_to(value, (ROWS, LANES))

            for slot in range(2):

                @pl.when(jnp.logical_not(is_near(chip_of(pair, slot))))
                def _():
                    at = pl.ds(pl.multiple_of((3 * pair + 2 * slot) * LANES, LANES), LANES)
                    for block in range(2):
                        green_high[block, :, at] = jnp.zeros((2 * qn, LANES), jnp.bfloat16)
                        green_low[block, :, at] = jnp.zeros((2 * qn, LANES), jnp.bfloat16)

            @pl.when(jnp.logical_not(pair_live(pair)))
            def _():
                at = pl.ds(pl.multiple_of((3 * pair + 1) * LANES, LANES), LANES)
                for block in range(2):
                    green_high[block, :, at] = jnp.zeros((2 * qn, LANES), jnp.bfloat16)
                    green_low[block, :, at] = jnp.zeros((2 * qn, LANES), jnp.bfloat16)

        @pl.when(mine)
        def _():
            own = place - 2 * first_pair
            green_of(3 * (own // 2) + 2 * lax.rem(own, 2), heads_of(snode_ref[...]))

        loads[6].wait()
        cols = columns_of(tgt_ref[...])
        for axis in range(6):
            line = cols[:, axis : axis + 1]
            if axis < 3:
                line = (line - first[:, axis : axis + 1]) * rate
            tgt_wide[axis] = jnp.broadcast_to(line, (2 * blk, LANES))
        loads[8].wait()
        for block in range(2):
            at = slice(block * blk, (block + 1) * blk)
            for part in range(2):
                tests[block, part * blk : (part + 1) * blk] = tweight_ref[part, :, at].T

    def pair_live(pair):
        return jnp.logical_or(is_near(chip_of(pair, 0)), is_near(chip_of(pair, 1)))

    def scaled(places):
        rate = wave_ref[0] * (0.5 / PI)
        return (places - origin[0:3]) * rate, rate * rate * (SOFT * SOFT)

    def green_of(chunk, places):
        places, soft = scaled(places)
        s_x, s_y, s_z = (jnp.broadcast_to(places[i : i + 1], (step_nodes, LANES)) for i in range(3))
        at = pl.ds(pl.multiple_of(chunk * LANES, LANES), LANES)

        @pl.loop(0, 2)
        def _(block):
            for group in range(ORDERS):
                here = slice(group * step_nodes, (group + 1) * step_nodes)
                scale = jnp.broadcast_to(scale_all[chunk * 2 + block, group, 0:1], (step_nodes, LANES))
                d_x = tnode_wide[block, 0, here] - s_x
                d_y = tnode_wide[block, 1, here] - s_y
                d_z = tnode_wide[block, 2, here] - s_z
                squared = d_x * d_x + d_y * d_y + (d_z * d_z + soft)
                inverse, cosine, u, sine = wave_parts(squared)
                inverse = inverse * scale
                for part, value in enumerate((inverse * cosine, (inverse * u) * sine)):
                    high, low = split_two(value)
                    to = slice(part * qn + group * step_nodes, part * qn + (group + 1) * step_nodes)
                    green_high[block, to, at] = high
                    green_low[block, to, at] = low

    urgent = n_row // 4

    @pl.when(jnp.logical_not(upper))
    def _():
        pack_bulk()
        prepare()

    pl.semaphore_wait(barrier, n_row)
    for_others(small_act("start"), 0, n_row)

    @pl.when(upper)
    def _():
        pack_bulk()

    for_others(bulk_act("start"), 0, urgent)

    @pl.when(upper)
    def _():
        prepare()

    for_others(bulk_act("start"), urgent, n_row)

    def wait_small(index):
        view = small_all.at[index]
        pltpu.make_async_copy(view, view, small_recv.at[index]).wait()

    def wait_bulk(index):
        near = is_near(2 * index + col)
        for planes, go in ((4, near), (1, jnp.logical_not(near))):

            @pl.when(go)
            def _():
                view = bulk_all.at[index, :, pl.ds(0, planes)]
                pltpu.make_async_copy(view, view, bulk_recv.at[index]).wait()

    @pl.loop(0, near_pairs)
    def _(turn):
        pair = near_pairs - 1 - turn
        base = 2 * (first_pair + pair)

        @pl.loop(0, 2)
        def _(slot):
            slot = 1 - slot
            wait_small(base + slot)
            chip = chip_of(pair, slot)

            @pl.when(jnp.logical_and(is_near(chip), chip != row))
            def _():
                green_of(3 * pair + 2 * slot, small_all[base + slot, 0, 0:3])

        @pl.when(pair_live(pair))
        def _():
            green_of(3 * pair + 1, small_all[base, 1, 0:3] + small_all[base + 1, 1, 0:3])

    def for_rest(act):
        if 2 * near_pairs < chips:

            @pl.loop(0, chips)
            def _(index):
                @pl.when(jnp.logical_or(index < 2 * first_pair, index >= 2 * (first_pair + near_pairs)))
                def _():
                    act(index)

    for_rest(wait_small)

    def impedance_of(chunk):
        packed = small_all[pl.ds(chunk * pieces, pieces), :, 4:8, :].reshape(2 * pieces, 4, LANES)
        packed = jnp.sum(packed, 0)
        places, soft = scaled(packed[0:3])
        area = packed[3:4] * (wave_ref[0] * (0.125 / PI / PI))
        at = pl.ds(pl.multiple_of(chunk * LANES, LANES), LANES)
        for part in range(4):
            block, half = part // 2, part % 2
            count = blk // 2
            here = slice(part * count, (part + 1) * count)
            d_x = tgt_wide[0, here] - places[0:1]
            d_y = tgt_wide[1, here] - places[1:2]
            d_z = tgt_wide[2, here] - places[2:3]
            squared = d_x * d_x + d_y * d_y + (d_z * d_z + soft)
            inverse, cosine, u, sine = wave_parts(squared)
            sine = u * sine
            along = tgt_wide[3, here] * d_x + tgt_wide[4, here] * d_y + tgt_wide[5, here] * d_z
            along = along * inverse
            scale = area * inverse
            green_re = scale * cosine
            green_im = scale * sine
            factor_re = 1.0 - along
            factor_im = along * (inverse * (-0.5 / PI))
            for side, value in enumerate(
                (
                    green_re * factor_re - green_im * factor_im,
                    green_re * factor_im + green_im * factor_re,
                )
            ):
                to = slice(side * blk + half * count, side * blk + (half + 1) * count)
                impedance[block, to, at] = value.astype(jnp.bfloat16)

    @pl.loop(0, chips // pieces)
    def _(chunk):
        impedance_of(chunk)

    @pl.loop(0, near_pairs)
    def _(pair):
        wait_bulk(2 * (first_pair + pair))
        wait_bulk(2 * (first_pair + pair) + 1)

    for slot in range(2 * near_pairs):
        index = 2 * first_pair + slot
        rows = bulk_all[index, :, 0].reshape(2 * per, width)
        weights = jnp.concatenate(
            [bulk_all[index, :, 1 + part].reshape(2 * per, LANES) for part in range(3)], 1
        )
        both = lax.dot_general(weights, rows, TN, preferred_element_type=jnp.float32)
        value = plus_i(both[:qn], both[qn:])
        value = jnp.where(is_near(2 * index + col), value, 0.0)
        high, low = split_two(value)
        at = slice((slot % 2) * qn, (slot % 2 + 1) * qn)
        moment[slot // 2, at, 0:width] = high
        moment[slot // 2, at, width:] = low

    for_rest(wait_bulk)

    def partial(block):
        def far_step(chunk, total):
            rows = bulk_all[pl.ds(chunk * pieces, pieces), :, 0].reshape(LANES, width)
            at = pl.ds(pl.multiple_of(chunk * LANES, LANES), LANES)
            return total + jnp.dot(impedance[block, :, at], rows, preferred_element_type=jnp.float32)

        right = moment[...].reshape(near_pairs * 2 * qn, 2 * width)
        both = jnp.dot(green_high[block], right, preferred_element_type=jnp.float32)
        both = both[:, :width] + both[:, width:]
        both = both + jnp.dot(green_low[block], right[:, :width], preferred_element_type=jnp.float32)
        high, low = split_two(plus_i(both[:qn], both[qn:]))
        product = jnp.dot(tests[block], jnp.concatenate([high, low], 1), preferred_element_type=jnp.float32)
        both = product[:, :width] + product[:, width:]
        if chips == pieces:
            both = far_step(0, both)
        else:
            both = lax.fori_loop(0, chips // pieces, far_step, both)
        return plus_i(both[:blk], both[blk:])

    swap = pltpu.make_async_remote_copy(
        src_ref=part_send,
        dst_ref=part_recv,
        send_sem=part_sem.at[0],
        recv_sem=part_sem.at[1],
        device_id={"col": 1 - col},
        device_id_type=MESH,
    )
    part_send[...] = partial(1 - col)
    swap.start()
    out_ref[...] = partial(col)
    for_others(small_act("wait_send"), 0, n_row)
    for_others(bulk_act("wait_send"), 0, n_row)
    swap.wait_recv()
    out_ref[...] += part_recv[...]
    swap.wait_send()


def on_device(
    wavenumber,
    tgt_geom,
    src_geom,
    excite,
    tgt_nodes,
    src_nodes,
    tgt_weights,
    src_weights,
    near_order,
):
    n_row = lax.axis_size("row")
    chips = n_row // 2
    blk = tgt_geom.shape[1] // 2
    qn = src_nodes.shape[1]
    per, width = src_geom.shape[1], excite.shape[0]
    excite_rows = excite.T
    weight_rows = src_weights.transpose(0, 2, 1)
    reach = (near_order.shape[1] - 1) // 2
    near_pairs = min(reach // 2 + 1, chips // 2)
    depth = near_pairs * 2 * qn
    hbm = pl.BlockSpec(memory_space=pl.ANY)
    dma = pltpu.SemaphoreType.DMA
    f32, bf16 = jnp.float32, jnp.bfloat16
    return pl.pallas_call(
        kernel,
        out_shape=pltpu.VMEM((blk, width), f32),
        in_specs=[hbm] * 9,
        out_specs=pl.BlockSpec(memory_space=pltpu.VMEM),
        scratch_shapes=[
            pltpu.VMEM((chips, 2, ROWS, LANES), f32),
            pltpu.VMEM((chips, 2, 4, per, LANES), bf16),
            pltpu.VMEM((ROWS, LANES), f32),
            pltpu.VMEM((4, per, LANES), bf16),
            pltpu.VMEM((2, 3, qn, LANES), f32),
            pltpu.VMEM((6, 2 * blk, LANES), f32),
            pltpu.VMEM((ROWS, LANES), f32),
            pltpu.VMEM((near_pairs * 6, ORDERS, ROWS, LANES), f32),
            pltpu.VMEM((2, 2 * blk, qn), bf16),
            pltpu.VMEM((2, 2 * qn, depth), bf16),
            pltpu.VMEM((2, 2 * qn, depth), bf16),
            pltpu.VMEM((near_pairs, 2 * qn, 2 * width), bf16),
            pltpu.VMEM((2, 2 * blk, chips * 2 * per), bf16),
            pltpu.VMEM((blk, width), f32),
            pltpu.VMEM((blk, width), f32),
            pltpu.SMEM(wavenumber.shape, f32),
            pltpu.SMEM(near_order.shape, jnp.int32),
            pltpu.VMEM(tgt_geom.shape, f32),
            pltpu.VMEM(tgt_nodes.shape, f32),
            pltpu.VMEM(tgt_weights.shape, bf16),
            pltpu.VMEM(src_geom.shape, f32),
            pltpu.VMEM(excite_rows.shape, bf16),
            pltpu.VMEM(src_nodes.shape, f32),
            pltpu.VMEM(weight_rows.shape, bf16),
            dma((9,)),
            dma((n_row,)),
            dma((n_row,)),
            dma((chips,)),
            dma((chips,)),
            dma((2,)),
        ],
        compiler_params=pltpu.CompilerParams(collective_id=0, has_side_effects=True),
        name="slab",
    )(
        wavenumber,
        near_order,
        tgt_geom,
        tgt_nodes,
        tgt_weights,
        src_geom,
        excite_rows,
        src_nodes,
        weight_rows,
    )


def solution(mesh):
    return jax.shard_map(
        on_device,
        mesh=mesh,
        in_specs=(
            P("groups"),
            P(None, ("groups", "row")),
            P(None, ("groups", "row", "col")),
            P(None, ("groups", "row", "col")),
            P(None, ("groups", "row")),
            P(None, ("groups", "row")),
            P(None, None, ("groups", "row")),
            P(None, None, ("groups", "row", "col")),
            P(("groups", "row"), None),
        ),
        out_specs=P(("groups", "row", "col"), None),
        check_vma=False,
    )
```

time: 15.3 us -> 14 us (0.915)
  Pallas kernels: 13.8 us -> 12.5 us
    pallas_call x1, Pallas kernels: 13.8 us -> 12.5 us  [on_device(): pl.pallas_call(kernel, out_shape=pltpu.VMEM((blk, width), f32), in_specs=...]
where the time goes in v4:
time: 14 us; the launch traced here: 13.8 us
  Pallas kernels  12.5 us (89%)
  between operations  0.66 us (5%)
  local copies, waits for them, and re-layouts  0.63 us (4%)
    pallas_call x1, Pallas kernels, on_device(): pl.pallas_call(kernel, out_shape=pltpu.VMEM((blk, width), f32), in_specs=...  12.5 us
    unnamed x1, local copies, waits for them, and re-layouts  0.63 us

profile of v4, /device:TPU:0, one launch (start us, length us, event | category | flops | bytes accessed | tf_op | source)
XLA Modules:
  0.0 13.8 jit_solution(13329648736954952485)
XLA Ops:
  0.7 12.5 %slab.1 = f32[128,128]{1,0:T(8,128)S(1)} custom-call(f32[1]{0:T(128)S(6)} %copy.12.wave_hbm, s32[2,9]{1,0:T(2,128)} %order_hbm.1, f32[6,256]{1,0:T(8,128)} %tgt_hbm.1, f32[3,384]{1,0:T(4,128)} %tnode_hbm.1, bf16[2,192,256]{2,1,0:T(8,128)(2,1)} %tweight_hbm.1, f32[4,16]{1,0:T(4,128)} %geom_hbm.1, bf16[16,128]{1,0:T(8,128)(2,1)} %bitcast.3, ...), custom_call_target="tpu_custom_call" | custom-call | tf_op jit(solution)/shard_map/slab/pallas_call | solution.py:535
  13.2 0.6 %copy.11 = f32[128,128]{1,0:T(8,128)} copy(f32[128,128]{1,0:T(8,128)S(1)} %slab.1) | data formatting | bytes 131072

commit v5 on v4

--- a/solution.py
+++ b/solution.py
@@ -101,6 +101,7 @@
     small_recv,
     bulk_recv,
     part_sem,
+    ready,
 ):
     n_row = lax.axis_size("row")
     row = lax.axis_index("row")
@@ -119,28 +120,7 @@
         (row - reach - col + 1 + 4 * reach) // 4 - reach, 0, chips // 2 - near_pairs
     )
     mine = home == col
-    upper = row >= chips
     lane = lax.broadcasted_iota(jnp.int32, (1, LANES), 1)
-
-    def outward(index, count):
-        return jnp.where(upper, index, count - 1 - index)
-
-    barrier = pltpu.get_barrier_semaphore()
-
-    @pl.loop(0, n_row)
-    def _(index):
-        index = outward(index, n_row)
-        chip, core = 2 * (index // 2) + col, lax.rem(index, 2)
-
-        @pl.when(jnp.logical_not(jnp.logical_and(chip == row, core == col)))
-        def _():
-            pl.semaphore_signal(
-                barrier, inc=1, device_id={"row": chip, "col": core}, device_id_type=MESH
-            )
-
-    @pl.when(jnp.logical_not(mine))
-    def _():
-        pl.semaphore_signal(barrier, inc=1, device_id={"col": 1 - col}, device_id_type=MESH)
 
     loads = [
         pltpu.make_async_copy(here, there, local.at[index])
@@ -161,6 +141,17 @@
     for load in loads:
         load.start()
 
+    barrier = pltpu.get_barrier_semaphore()
+
+    @pl.loop(2 * row + col + 1, 2 * n_row)
+    def _(index):
+        pl.semaphore_signal(
+            barrier,
+            inc=1,
+            device_id={"row": index // 2, "col": lax.rem(index, 2)},
+            device_id_type=MESH,
+        )
+
     def heads_of(nodes):
         return jnp.where(lax.rem(place, 2) == 0, nodes[:, :LANES], nodes[:, tail:])
 
@@ -222,12 +213,39 @@
     def is_near(chip):
         return jnp.logical_and(chip >= row - reach, chip <= row + reach)
 
+    lower_end = row + jnp.where(home < col, 1, 0)
+    higher_begin = row + jnp.where(home > col, 0, 1)
+
     def for_others(act, begin, end):
         @pl.loop(begin, end)
         def _(chip):
             @pl.when(jnp.logical_not(jnp.logical_and(mine, chip == row)))
             def _():
                 act(chip)
+
+    def tell(chip, core, slot):
+        pl.semaphore_signal(
+            ready.at[slot], inc=1, device_id={"row": chip, "col": core}, device_id_type=MESH
+        )
+
+    def tell_lower():
+        @pl.loop(0, row // 2 + 1)
+        def _(index):
+            chip = 2 * index + col
+            for core in range(2):
+
+                @pl.when(2 * chip + core < 2 * row + col)
+                def _():
+                    tell(chip, core, row)
+
+        @pl.when(jnp.logical_and(col == 1, home == 0))
+        def _():
+            tell(row, 0, n_row)
+
+    def send_higher(chip):
+        pl.semaphore_wait(ready.at[chip], 1)
+        small_to(chip).start()
+        bulk_act("start")(chip)
 
     def small_act(name):
         return lambda chip: getattr(small_to(chip), name)()
@@ -349,27 +367,20 @@
                     green_high[block, to, at] = high
                     green_low[block, to, at] = low
 
-    urgent = n_row // 4
-
-    @pl.when(jnp.logical_not(upper))
+    @pl.when(2 * row + col > 0)
     def _():
-        pack_bulk()
-        prepare()
-
-    pl.semaphore_wait(barrier, n_row)
-    for_others(small_act("start"), 0, n_row)
-
-    @pl.when(upper)
+        pl.semaphore_wait(barrier, 2 * row + col)
+
+    tell_lower()
+    for_others(small_act("start"), 0, lower_end)
+    pack_bulk()
+    for_others(bulk_act("start"), 0, lower_end)
+    prepare()
+    for_others(send_higher, higher_begin, n_row)
+
+    @pl.when(jnp.logical_and(col == 0, home == 0))
     def _():
-        pack_bulk()
-
-    for_others(bulk_act("start"), 0, urgent)
-
-    @pl.when(upper)
-    def _():
-        prepare()
-
-    for_others(bulk_act("start"), urgent, n_row)
+        pl.semaphore_wait(ready.at[n_row], 1)
 
     def wait_small(index):
         view = small_all.at[index]
@@ -568,6 +579,7 @@
             dma((chips,)),
             dma((chips,)),
             dma((2,)),
+            pltpu.SemaphoreType.REGULAR((n_row + 1,)),
         ],
         compiler_params=pltpu.CompilerParams(collective_id=0, has_side_effects=True),
         name="slab",

time: 14 us -> 13.7 us (0.979)
  Pallas kernels: 12.5 us -> 12.2 us
    pallas_call x1, Pallas kernels: 12.5 us -> 12.2 us  [on_device(): pl.pallas_call(kernel, out_shape=pltpu.VMEM((blk, width), f32), in_specs=...]
where the time goes in v5:
time: 13.7 us; the launch traced here: 13.5 us
  Pallas kernels  12.2 us (89%)
  between operations  0.66 us (5%)
  local copies, waits for them, and re-layouts  0.63 us (5%)
    pallas_call x1, Pallas kernels, on_device(): pl.pallas_call(kernel, out_shape=pltpu.VMEM((blk, width), f32), in_specs=...  12.2 us
    unnamed x1, local copies, waits for them, and re-layouts  0.63 us

profile of v5, /device:TPU:0, one launch (start us, length us, event | category | flops | bytes accessed | tf_op | source)
XLA Modules:
  0.0 13.5 jit_solution(1593027377674238735)
XLA Ops:
  0.7 12.2 %slab.1 = f32[128,128]{1,0:T(8,128)S(1)} custom-call(f32[1]{0:T(128)S(6)} %copy.12.wave_hbm, s32[2,9]{1,0:T(2,128)} %order_hbm.1, f32[6,256]{1,0:T(8,128)} %tgt_hbm.1, f32[3,384]{1,0:T(4,128)} %tnode_hbm.1, bf16[2,192,256]{2,1,0:T(8,128)(2,1)} %tweight_hbm.1, f32[4,16]{1,0:T(4,128)} %geom_hbm.1, bf16[16,128]{1,0:T(8,128)(2,1)} %bitcast.3, ...), custom_call_target="tpu_custom_call" | custom-call | tf_op jit(solution)/shard_map/slab/pallas_call | solution.py:546
  12.9 0.6 %copy.11 = f32[128,128]{1,0:T(8,128)} copy(f32[128,128]{1,0:T(8,128)S(1)} %slab.1) | data formatting | bytes 131072

commit v6 on v5

--- a/solution.py
+++ b/solution.py
@@ -73,6 +73,8 @@
     out_ref,
     small_all,
     bulk_all,
+    far_all,
+    middle,
     small_pack,
     bulk_pack,
     tnode_wide,
@@ -200,10 +202,10 @@
             device_id_type=MESH,
         )
 
-    def bulk_to(chip, planes):
+    def bulk_to(chip, near):
         return pltpu.make_async_remote_copy(
-            src_ref=bulk_pack.at[pl.ds(0, planes)],
-            dst_ref=bulk_all.at[place, col, pl.ds(0, planes)],
+            src_ref=bulk_pack if near else bulk_pack.at[0],
+            dst_ref=bulk_all.at[place, col] if near else far_all.at[place, col],
             send_sem=bulk_send.at[chip],
             recv_sem=bulk_recv.at[place],
             device_id={"row": chip, "col": home},
@@ -256,11 +258,11 @@
 
             @pl.when(near)
             def _():
-                getattr(bulk_to(chip, 4), name)()
+                getattr(bulk_to(chip, True), name)()
 
             @pl.when(jnp.logical_not(near))
             def _():
-                getattr(bulk_to(chip, 1), name)()
+                getattr(bulk_to(chip, False), name)()
 
         return act
 
@@ -388,23 +390,30 @@
 
     def wait_bulk(index):
         near = is_near(2 * index + col)
-        for planes, go in ((4, near), (1, jnp.logical_not(near))):
+        for view, go in ((bulk_all.at[index], near), (far_all.at[index], jnp.logical_not(near))):
 
             @pl.when(go)
             def _():
-                view = bulk_all.at[index, :, pl.ds(0, planes)]
                 pltpu.make_async_copy(view, view, bulk_recv.at[index]).wait()
+
+    def inward(index, count):
+        return jnp.where(row < chips, index, count - 1 - index)
 
     @pl.loop(0, near_pairs)
     def _(turn):
-        pair = near_pairs - 1 - turn
+        pair = inward(turn, near_pairs)
         base = 2 * (first_pair + pair)
+        middle[0:3] = jnp.zeros((3, LANES), jnp.float32)
 
         @pl.loop(0, 2)
         def _(slot):
-            slot = 1 - slot
-            wait_small(base + slot)
+            slot = inward(slot, 2)
             chip = chip_of(pair, slot)
+
+            @pl.when(is_near(chip))
+            def _():
+                wait_small(base + slot)
+                middle[0:3] += small_all[base + slot, 1, 0:3]
 
             @pl.when(jnp.logical_and(is_near(chip), chip != row))
             def _():
@@ -412,18 +421,16 @@
 
         @pl.when(pair_live(pair))
         def _():
-            green_of(3 * pair + 1, small_all[base, 1, 0:3] + small_all[base + 1, 1, 0:3])
-
-    def for_rest(act):
-        if 2 * near_pairs < chips:
-
-            @pl.loop(0, chips)
-            def _(index):
-                @pl.when(jnp.logical_or(index < 2 * first_pair, index >= 2 * (first_pair + near_pairs)))
-                def _():
-                    act(index)
-
-    for_rest(wait_small)
+            green_of(3 * pair + 1, middle[0:3])
+
+    def for_chips(act, near):
+        @pl.loop(0, chips)
+        def _(index):
+            go = is_near(2 * index + col)
+
+            @pl.when(go if near else jnp.logical_not(go))
+            def _():
+                act(index)
 
     def impedance_of(chunk):
         packed = small_all[pl.ds(chunk * pieces, pieces), :, 4:8, :].reshape(2 * pieces, 4, LANES)
@@ -457,14 +464,7 @@
                 to = slice(side * blk + half * count, side * blk + (half + 1) * count)
                 impedance[block, to, at] = value.astype(jnp.bfloat16)
 
-    @pl.loop(0, chips // pieces)
-    def _(chunk):
-        impedance_of(chunk)
-
-    @pl.loop(0, near_pairs)
-    def _(pair):
-        wait_bulk(2 * (first_pair + pair))
-        wait_bulk(2 * (first_pair + pair) + 1)
+    for_chips(wait_bulk, True)
 
     for slot in range(2 * near_pairs):
         index = 2 * first_pair + slot
@@ -480,21 +480,30 @@
         moment[slot // 2, at, 0:width] = high
         moment[slot // 2, at, width:] = low
 
-    for_rest(wait_bulk)
-
-    def partial(block):
-        def far_step(chunk, total):
-            rows = bulk_all[pl.ds(chunk * pieces, pieces), :, 0].reshape(LANES, width)
-            at = pl.ds(pl.multiple_of(chunk * LANES, LANES), LANES)
-            return total + jnp.dot(impedance[block, :, at], rows, preferred_element_type=jnp.float32)
-
+    def near_part(block):
         right = moment[...].reshape(near_pairs * 2 * qn, 2 * width)
         both = jnp.dot(green_high[block], right, preferred_element_type=jnp.float32)
         both = both[:, :width] + both[:, width:]
         both = both + jnp.dot(green_low[block], right[:, :width], preferred_element_type=jnp.float32)
         high, low = split_two(plus_i(both[:qn], both[qn:]))
         product = jnp.dot(tests[block], jnp.concatenate([high, low], 1), preferred_element_type=jnp.float32)
-        both = product[:, :width] + product[:, width:]
+        return product[:, :width] + product[:, width:]
+
+    def far_part(block, both):
+        def far_step(chunk, total):
+            rows = []
+            for piece in range(pieces):
+                index = chunk * pieces + piece
+                rows.append(
+                    jnp.where(is_near(2 * index + col), bulk_all[index, :, 0], far_all[index]).reshape(
+                        2 * per, width
+                    )
+                )
+            at = pl.ds(pl.multiple_of(chunk * LANES, LANES), LANES)
+            return total + jnp.dot(
+                impedance[block, :, at], jnp.concatenate(rows, 0), preferred_element_type=jnp.float32
+            )
+
         if chips == pieces:
             both = far_step(0, both)
         else:
@@ -509,9 +518,17 @@
         device_id={"col": 1 - col},
         device_id_type=MESH,
     )
-    part_send[...] = partial(1 - col)
+    other = near_part(1 - col)
+    for_chips(wait_small, False)
+    for_chips(wait_bulk, False)
+
+    @pl.loop(0, chips // pieces)
+    def _(chunk):
+        impedance_of(chunk)
+
+    part_send[...] = far_part(1 - col, other)
     swap.start()
-    out_ref[...] = partial(col)
+    out_ref[...] = far_part(col, near_part(col))
     for_others(small_act("wait_send"), 0, n_row)
     for_others(bulk_act("wait_send"), 0, n_row)
     swap.wait_recv()
@@ -551,6 +568,8 @@
         scratch_shapes=[
             pltpu.VMEM((chips, 2, ROWS, LANES), f32),
             pltpu.VMEM((chips, 2, 4, per, LANES), bf16),
+            pltpu.VMEM((chips, 2, per, LANES), bf16),
+            pltpu.VMEM((ROWS, LANES), f32),
             pltpu.VMEM((ROWS, LANES), f32),
             pltpu.VMEM((4, per, LANES), bf16),
             pltpu.VMEM((2, 3, qn, LANES), f32),

time: 13.7 us -> 12.9 us (0.942)
  Pallas kernels: 12.2 us -> 11.4 us
    pallas_call x1, Pallas kernels: 12.2 us -> 11.4 us  [on_device(): pl.pallas_call(kernel, out_shape=pltpu.VMEM((blk, width), f32), in_specs=...]
where the time goes in v6:
time: 12.9 us; the launch traced here: 12.7 us
  Pallas kernels  11.4 us (88%)
  between operations  0.66 us (5%)
  local copies, waits for them, and re-layouts  0.63 us (5%)
    pallas_call x1, Pallas kernels, on_device(): pl.pallas_call(kernel, out_shape=pltpu.VMEM((blk, width), f32), in_specs=...  11.4 us
    unnamed x1, local copies, waits for them, and re-layouts  0.63 us

profile of v6, /device:TPU:0, one launch (start us, length us, event | category | flops | bytes accessed | tf_op | source)
XLA Modules:
  0.0 12.7 jit_solution(3482740691333810688)
XLA Ops:
  0.7 11.4 %slab.1 = f32[128,128]{1,0:T(8,128)S(1)} custom-call(f32[1]{0:T(128)S(6)} %copy.12.wave_hbm, s32[2,9]{1,0:T(2,128)} %order_hbm.1, f32[6,256]{1,0:T(8,128)} %tgt_hbm.1, f32[3,384]{1,0:T(4,128)} %tnode_hbm.1, bf16[2,192,256]{2,1,0:T(8,128)(2,1)} %tweight_hbm.1, f32[4,16]{1,0:T(4,128)} %geom_hbm.1, bf16[16,128]{1,0:T(8,128)(2,1)} %bitcast.3, ...), custom_call_target="tpu_custom_call" | custom-call | tf_op jit(solution)/shard_map/slab/pallas_call | solution.py:563
  12.1 0.6 %copy.11 = f32[128,128]{1,0:T(8,128)} copy(f32[128,128]{1,0:T(8,128)S(1)} %slab.1) | data formatting | bytes 131072

commit v7 on v6

--- a/solution.py
+++ b/solution.py
@@ -464,7 +464,15 @@
                 to = slice(side * blk + half * count, side * blk + (half + 1) * count)
                 impedance[block, to, at] = value.astype(jnp.bfloat16)
 
-    for_chips(wait_bulk, True)
+    for_chips(wait_small, False)
+
+    @pl.loop(0, chips // pieces)
+    def _(chunk):
+        impedance_of(chunk)
+
+    @pl.loop(0, chips)
+    def _(index):
+        wait_bulk(index)
 
     for slot in range(2 * near_pairs):
         index = 2 * first_pair + slot
@@ -518,15 +526,7 @@
         device_id={"col": 1 - col},
         device_id_type=MESH,
     )
-    other = near_part(1 - col)
-    for_chips(wait_small, False)
-    for_chips(wait_bulk, False)
-
-    @pl.loop(0, chips // pieces)
-    def _(chunk):
-        impedance_of(chunk)
-
-    part_send[...] = far_part(1 - col, other)
+    part_send[...] = far_part(1 - col, near_part(1 - col))
     swap.start()
     out_ref[...] = far_part(col, near_part(col))
     for_others(small_act("wait_send"), 0, n_row)

time: 12.9 us -> 12.6 us (0.977)
  Pallas kernels: 11.4 us -> 11.1 us
    pallas_call x1, Pallas kernels: 11.4 us -> 11.1 us  [on_device(): pl.pallas_call(kernel, out_shape=pltpu.VMEM((blk, width), f32), in_specs=...]
where the time goes in v7:
time: 12.6 us; the launch traced here: 12.4 us
  Pallas kernels  11.1 us (88%)
  between operations  0.66 us (5%)
  local copies, waits for them, and re-layouts  0.63 us (5%)
    pallas_call x1, Pallas kernels, on_device(): pl.pallas_call(kernel, out_shape=pltpu.VMEM((blk, width), f32), in_specs=...  11.1 us
    unnamed x1, local copies, waits for them, and re-layouts  0.63 us

profile of v7, /device:TPU:0, one launch (start us, length us, event | category | flops | bytes accessed | tf_op | source)
XLA Modules:
  0.0 12.4 jit_solution(10807878887593346906)
XLA Ops:
  0.7 11.1 %slab.1 = f32[128,128]{1,0:T(8,128)S(1)} custom-call(f32[1]{0:T(128)S(6)} %copy.12.wave_hbm, s32[2,9]{1,0:T(2,128)} %order_hbm.1, f32[6,256]{1,0:T(8,128)} %tgt_hbm.1, f32[3,384]{1,0:T(4,128)} %tnode_hbm.1, bf16[2,192,256]{2,1,0:T(8,128)(2,1)} %tweight_hbm.1, f32[4,16]{1,0:T(4,128)} %geom_hbm.1, bf16[16,128]{1,0:T(8,128)(2,1)} %bitcast.3, ...), custom_call_target="tpu_custom_call" | custom-call | tf_op jit(solution)/shard_map/slab/pallas_call | solution.py:563
  11.8 0.6 %copy.11 = f32[128,128]{1,0:T(8,128)} copy(f32[128,128]{1,0:T(8,128)S(1)} %slab.1) | data formatting | bytes 131072

commit v8 on v7

--- a/solution.py
+++ b/solution.py
@@ -374,10 +374,12 @@
         pl.semaphore_wait(barrier, 2 * row + col)
 
     tell_lower()
+    urgent = jnp.minimum(lower_end, 2)
     for_others(small_act("start"), 0, lower_end)
     pack_bulk()
-    for_others(bulk_act("start"), 0, lower_end)
+    for_others(bulk_act("start"), 0, urgent)
     prepare()
+    for_others(bulk_act("start"), urgent, lower_end)
     for_others(send_higher, higher_begin, n_row)
 
     @pl.when(jnp.logical_and(col == 0, home == 0))

time: 12.6 us -> 12.5 us (level)
  no operation moved by 1% of the time
where the time goes in v8:
time: 12.5 us; the launch traced here: 12.3 us
  Pallas kernels  11 us (88%)
  between operations  0.66 us (5%)
  local copies, waits for them, and re-layouts  0.63 us (5%)
    pallas_call x1, Pallas kernels, on_device(): pl.pallas_call(kernel, out_shape=pltpu.VMEM((blk, width), f32), in_specs=...  11 us
    unnamed x1, local copies, waits for them, and re-layouts  0.63 us

profile of v8, /device:TPU:0, one launch (start us, length us, event | category | flops | bytes accessed | tf_op | source)
XLA Modules:
  0.0 12.3 jit_solution(2766664016198165028)
XLA Ops:
  0.7 11.0 %slab.1 = f32[128,128]{1,0:T(8,128)S(1)} custom-call(f32[1]{0:T(128)S(6)} %copy.12.wave_hbm, s32[2,9]{1,0:T(2,128)} %order_hbm.1, f32[6,256]{1,0:T(8,128)} %tgt_hbm.1, f32[3,384]{1,0:T(4,128)} %tnode_hbm.1, bf16[2,192,256]{2,1,0:T(8,128)(2,1)} %tweight_hbm.1, f32[4,16]{1,0:T(4,128)} %geom_hbm.1, bf16[16,128]{1,0:T(8,128)(2,1)} %bitcast.3, ...), custom_call_target="tpu_custom_call" | custom-call | tf_op jit(solution)/shard_map/slab/pallas_call | solution.py:565
  11.7 0.6 %copy.11 = f32[128,128]{1,0:T(8,128)} copy(f32[128,128]{1,0:T(8,128)S(1)} %slab.1) | data formatting | bytes 131072

commit v9 on v8

--- a/solution.py
+++ b/solution.py
@@ -369,61 +369,75 @@
                     green_high[block, to, at] = high
                     green_low[block, to, at] = low
 
+    pack_bulk()
+
     @pl.when(2 * row + col > 0)
     def _():
         pl.semaphore_wait(barrier, 2 * row + col)
 
     tell_lower()
-    urgent = jnp.minimum(lower_end, 2)
-    for_others(small_act("start"), 0, lower_end)
-    pack_bulk()
-    for_others(bulk_act("start"), 0, urgent)
+    urgent = jnp.minimum(lower_end, jnp.maximum(row - reach, 2))
+
+    def both_act(chip):
+        small_to(chip).start()
+        bulk_act("start")(chip)
+
+    for_others(both_act, 0, urgent)
+    for_others(small_act("start"), urgent, lower_end)
     prepare()
     for_others(bulk_act("start"), urgent, lower_end)
-    for_others(send_higher, higher_begin, n_row)
+    split = jnp.where(row == 0, jnp.minimum(reach + 2, n_row), n_row)
+    for_others(send_higher, higher_begin, split)
+
+    def wait_small(index):
+        view = small_all.at[index]
+        pltpu.make_async_copy(view, view, small_recv.at[index]).wait()
+
+    def wait_bulk(index):
+        near = is_near(2 * index + col)
+        for view, go in ((bulk_all.at[index], near), (far_all.at[index], jnp.logical_not(near))):
+
+            @pl.when(go)
+            def _():
+                pltpu.make_async_copy(view, view, bulk_recv.at[index]).wait()
+
+    def inward(index, count):
+        return jnp.where(row < chips, index, count - 1 - index)
+
+    def green_some(begin, end):
+        @pl.loop(begin, end)
+        def _(turn):
+            pair = inward(turn, near_pairs)
+            base = 2 * (first_pair + pair)
+            middle[0:3] = jnp.zeros((3, LANES), jnp.float32)
+
+            @pl.loop(0, 2)
+            def _(slot):
+                slot = inward(slot, 2)
+                chip = chip_of(pair, slot)
+
+                @pl.when(is_near(chip))
+                def _():
+                    wait_small(base + slot)
+                    middle[0:3] += small_all[base + slot, 1, 0:3]
+
+                @pl.when(jnp.logical_and(is_near(chip), chip != row))
+                def _():
+                    green_of(3 * pair + 2 * slot, small_all[base + slot, 0, 0:3])
+
+            @pl.when(pair_live(pair))
+            def _():
+                green_of(3 * pair + 1, middle[0:3])
+
+    done = jnp.where(row == 0, 1, 0)
+    green_some(0, done)
+    for_others(send_higher, split, n_row)
 
     @pl.when(jnp.logical_and(col == 0, home == 0))
     def _():
         pl.semaphore_wait(ready.at[n_row], 1)
 
-    def wait_small(index):
-        view = small_all.at[index]
-        pltpu.make_async_copy(view, view, small_recv.at[index]).wait()
-
-    def wait_bulk(index):
-        near = is_near(2 * index + col)
-        for view, go in ((bulk_all.at[index], near), (far_all.at[index], jnp.logical_not(near))):
-
-            @pl.when(go)
-            def _():
-                pltpu.make_async_copy(view, view, bulk_recv.at[index]).wait()
-
-    def inward(index, count):
-        return jnp.where(row < chips, index, count - 1 - index)
-
-    @pl.loop(0, near_pairs)
-    def _(turn):
-        pair = inward(turn, near_pairs)
-        base = 2 * (first_pair + pair)
-        middle[0:3] = jnp.zeros((3, LANES), jnp.float32)
-
-        @pl.loop(0, 2)
-        def _(slot):
-            slot = inward(slot, 2)
-            chip = chip_of(pair, slot)
-
-            @pl.when(is_near(chip))
-            def _():
-                wait_small(base + slot)
-                middle[0:3] += small_all[base + slot, 1, 0:3]
-
-            @pl.when(jnp.logical_and(is_near(chip), chip != row))
-            def _():
-                green_of(3 * pair + 2 * slot, small_all[base + slot, 0, 0:3])
-
-        @pl.when(pair_live(pair))
-        def _():
-            green_of(3 * pair + 1, middle[0:3])
+    green_some(done, near_pairs)
 
     def for_chips(act, near):
         @pl.loop(0, chips)

time: 12.5 us -> 12.5 us (level)
  no operation moved by 1% of the time
where the time goes in v9:
time: 12.5 us; the launch traced here: 12.3 us
  Pallas kernels  11 us (88%)
  between operations  0.66 us (5%)
  local copies, waits for them, and re-layouts  0.63 us (5%)
    pallas_call x1, Pallas kernels, on_device(): pl.pallas_call(kernel, out_shape=pltpu.VMEM((blk, width), f32), in_specs=...  11 us
    unnamed x1, local copies, waits for them, and re-layouts  0.63 us

profile of v9, /device:TPU:0, one launch (start us, length us, event | category | flops | bytes accessed | tf_op | source)
XLA Modules:
  0.0 12.3 jit_solution(2150385169350920224)
XLA Ops:
  0.7 11.0 %slab.1 = f32[128,128]{1,0:T(8,128)S(1)} custom-call(f32[1]{0:T(128)S(6)} %copy.12.wave_hbm, s32[2,9]{1,0:T(2,128)} %order_hbm.1, f32[6,256]{1,0:T(8,128)} %tgt_hbm.1, f32[3,384]{1,0:T(4,128)} %tnode_hbm.1, bf16[2,192,256]{2,1,0:T(8,128)(2,1)} %tweight_hbm.1, f32[4,16]{1,0:T(4,128)} %geom_hbm.1, bf16[16,128]{1,0:T(8,128)(2,1)} %bitcast.3, ...), custom_call_target="tpu_custom_call" | custom-call | tf_op jit(solution)/shard_map/slab/pallas_call | solution.py:579
  11.7 0.6 %copy.11 = f32[128,128]{1,0:T(8,128)} copy(f32[128,128]{1,0:T(8,128)S(1)} %slab.1) | data formatting | bytes 131072

commit v10 on v9

--- a/solution.py
+++ b/solution.py
@@ -23,8 +23,8 @@
     return [float(c) for c in np.linalg.solve(matrix, function(np.sqrt(nodes)))]
 
 
-COS = fitted(lambda u: np.cos(2.0 * np.pi * u), 6)
-SIN = fitted(lambda u: np.sin(2.0 * np.pi * u) / u, 6)
+HALF_COS = fitted(lambda u: math.sqrt(2.0) * np.cos(np.pi * u), 5)
+HALF_SIN = fitted(lambda u: math.sqrt(2.0) * np.sin(np.pi * u) / u, 4)
 
 
 def horner(coefficients, y):
@@ -39,7 +39,8 @@
     turns = squared * inverse
     u = turns - jnp.round(turns)
     y = u * u
-    return inverse, horner(COS, y), u, horner(SIN, y)
+    half = u * horner(HALF_SIN, y)
+    return inverse, 1.0 - half * half, half * horner(HALF_COS, y)
 
 
 def plus_i(first, second):
@@ -361,9 +362,9 @@
                 d_y = tnode_wide[block, 1, here] - s_y
                 d_z = tnode_wide[block, 2, here] - s_z
                 squared = d_x * d_x + d_y * d_y + (d_z * d_z + soft)
-                inverse, cosine, u, sine = wave_parts(squared)
+                inverse, cosine, sine = wave_parts(squared)
                 inverse = inverse * scale
-                for part, value in enumerate((inverse * cosine, (inverse * u) * sine)):
+                for part, value in enumerate((inverse * cosine, inverse * sine)):
                     high, low = split_two(value)
                     to = slice(part * qn + group * step_nodes, part * qn + (group + 1) * step_nodes)
                     green_high[block, to, at] = high
@@ -462,8 +463,7 @@
             d_y = tgt_wide[1, here] - places[1:2]
             d_z = tgt_wide[2, here] - places[2:3]
             squared = d_x * d_x + d_y * d_y + (d_z * d_z + soft)
-            inverse, cosine, u, sine = wave_parts(squared)
-            sine = u * sine
+            inverse, cosine, sine = wave_parts(squared)
             along = tgt_wide[3, here] * d_x + tgt_wide[4, here] * d_y + tgt_wide[5, here] * d_z
             along = along * inverse
             scale = area * inverse

time: 12.5 us -> 12.5 us (level)
  no operation moved by 1% of the time
where the time goes in v10:
time: 12.5 us; the launch traced here: 12.3 us
  Pallas kernels  11 us (88%)
  between operations  0.66 us (5%)
  local copies, waits for them, and re-layouts  0.63 us (5%)
    pallas_call x1, Pallas kernels, on_device(): pl.pallas_call(kernel, out_shape=pltpu.VMEM((blk, width), f32), in_specs=...  11 us
    unnamed x1, local copies, waits for them, and re-layouts  0.63 us

profile of v10, /device:TPU:0, one launch (start us, length us, event | category | flops | bytes accessed | tf_op | source)
XLA Modules:
  0.0 12.3 jit_solution(18025726255161300124)
XLA Ops:
  0.7 11.0 %slab.1 = f32[128,128]{1,0:T(8,128)S(1)} custom-call(f32[1]{0:T(128)S(6)} %copy.12.wave_hbm, s32[2,9]{1,0:T(2,128)} %order_hbm.1, f32[6,256]{1,0:T(8,128)} %tgt_hbm.1, f32[3,384]{1,0:T(4,128)} %tnode_hbm.1, bf16[2,192,256]{2,1,0:T(8,128)(2,1)} %tweight_hbm.1, f32[4,16]{1,0:T(4,128)} %geom_hbm.1, bf16[16,128]{1,0:T(8,128)(2,1)} %bitcast.3, ...), custom_call_target="tpu_custom_call" | custom-call | tf_op jit(solution)/shard_map/slab/pallas_call | solution.py:579
  11.7 0.6 %copy.11 = f32[128,128]{1,0:T(8,128)} copy(f32[128,128]{1,0:T(8,128)S(1)} %slab.1) | data formatting | bytes 131072
